TPU v7x, 1024 devices: a whole 4x8x16 slice. The times are simulated.
1024 devices in a mesh: gx: 16 (over z), gy: 16 (over y, core), gz: 4 (over x).
Axes of the slice: x: 4, y: 8, z: 16, core: 2. Of those that a mesh axis runs over, the one named last changes fastest.
Arguments:
- positions: float32 [3, 32, 32, 8, 128], P(None, 'gx', 'gy', 'gz'), may hold values from 0 to 12
- charges: float32 [32, 32, 8, 128], P('gx', 'gy', 'gz'), may hold values from -3 to 3
- atom_types: int32 [32, 32, 8, 128], P('gx', 'gy', 'gz'), may hold values from 0 to 127
- atom_counts: int32 [32, 32, 8], P('gx', 'gy', 'gz'), may hold values from 48 to 128, as said below
- type_sigma: float32 [128], replicated, may hold values from 1 to 3.2
- type_epsilon: float32 [128], replicated, may hold values from 0.02 to 0.5
- pair_list: int32 [2, 16, 16, 4, 188], P(None, 'gx', 'gy', 'gz'), may hold values from -1 to 26, as said below
Outputs:
- forces: float32 [3, 32, 32, 8, 128], P(None, 'gx', 'gy', 'gz')
Inputs may be any that keep to these rules, and one draw needn't show every extreme that they name: The first atom_counts[c] slots of cell c hold atoms; some cell holds 128. `pair_list`: row 0 holds a local cell index below 8, row 1 a neighbour code of 0 to 26 or -1 for an empty slot; empty slots come after the listed ones. Over all blocks each cell is listed with itself (code 13) exactly once, and each unordered pair of distinct neighbouring cells at most once; pairs that the list leaves out are not computed. Some block lists exactly 188 pairs.
All inputs are finite; a program needn't handle non-finite values.
Results may differ from a plain program's by a relative error of at most 0.0003.
Values sent between devices are 32-bit elements; how exact they have to be, the bound alone decides.
No kernel may reach another device: no remote copies, remote signals or barrier semaphores. Data moves between devices by JAX's collectives and lax.ppermute only.
A program may use at most 32 MiB of HBM per device.

v0:
```python
import jax
import jax.numpy as jnp
from jax import lax
from jax.sharding import PartitionSpec as P

cell_edge = 12.0
switch_on = 100.0
cutoff_sq = 144.0
switch_den = 44.0 * 44.0 * 44.0
block_pairs = 12


def padded_2(shard, sides, width):
    for axis, dim in sides:
        size, length = (lax.axis_size(axis), shard.shape[dim])
        up = [(i, (i + 1) % size) for i in range(size)]
        down = [(j, i) for i, j in up]
        last = lax.slice_in_dim(shard, length - width, length, axis=dim)
        leading = lax.slice_in_dim(shard, 0, width, axis=dim)
        before = lax.ppermute(last, axis, up)
        after = lax.ppermute(leading, axis, down)
        shard = jnp.concatenate([before, shard, after], axis=dim)
    return shard


def table_lookup(type_codes, live_slots, type_sigma, root_depth):
    catalog = jnp.arange(type_sigma.shape[0])
    matches = type_codes[..., None] == catalog
    sigma_atom = jnp.where(live_slots, jnp.sum(jnp.where(matches, type_sigma, 0.0), -1), 1.0)
    depth_atom = jnp.where(live_slots, jnp.sum(jnp.where(matches, root_depth, 0.0), -1), 0.0)
    return (sigma_atom, depth_atom)


def decode(code_ids):
    valid_slot = code_ids >= 0
    safe_code = jnp.where(valid_slot, code_ids, 13)
    move_first = safe_code // 9 - 1
    move_second = safe_code // 3 % 3 - 1
    move_third = safe_code % 3 - 1
    weight = jnp.where(valid_slot, jnp.where(safe_code == 13, 0.5, 1.0), 0.0)
    return (move_first, move_second, move_third, weight)


def pair_forces(left_atoms, right_atoms, offset):
    separation = [
        left_atoms[component][:, :, None]
        - right_atoms[component][:, None, :]
        + offset[component][:, None, None]
        for component in range(3)
    ]
    dist_sq = (
        separation[0] * separation[0]
        + separation[1] * separation[1]
        + separation[2] * separation[2]
    )
    sigma_mean = 0.5 * (left_atoms[4][:, :, None] + right_atoms[4][:, None, :])
    sigma_sq = sigma_mean * sigma_mean
    soft_sq = dist_sq + sigma_sq
    inverse = 1.0 / soft_sq
    size_ratio = sigma_sq * inverse
    third_power = size_ratio * size_ratio * size_ratio
    well_depth = 4.0 * left_atoms[5][:, :, None] * right_atoms[5][:, None, :]
    coulomb = left_atoms[3][:, :, None] * right_atoms[3][:, None, :] * lax.rsqrt(soft_sq)
    energy = well_depth * (third_power * third_power - third_power) + coulomb
    energy_slope = (
        well_depth * (3.0 * third_power - 6.0 * third_power * third_power) - 0.5 * coulomb
    ) * inverse
    clipped = jnp.clip(dist_sq, switch_on, cutoff_sq)
    switch = (
        (cutoff_sq - clipped)
        * (cutoff_sq - clipped)
        * (cutoff_sq + 2.0 * clipped - 3.0 * switch_on)
        / switch_den
    )
    switch_slope = 6.0 * (cutoff_sq - clipped) * (switch_on - clipped) / switch_den
    pair_scale = -2.0 * (switch_slope * energy + switch * energy_slope)
    on_left = jnp.stack([jnp.sum(pair_scale * component, 2) for component in separation])
    on_right = -jnp.stack([jnp.sum(pair_scale * component, 1) for component in separation])
    return (on_left, on_right)


def edge_rims(forces, dim):
    size_dim = forces.shape[dim]
    lower_rim = lax.slice_in_dim(forces, 0, 1, axis=dim)
    upper_rim = lax.slice_in_dim(forces, size_dim - 1, size_dim, axis=dim)
    return jnp.concatenate([lower_rim, upper_rim], dim)


def settle(forces, dim, arrived):
    size_dim = forces.shape[dim]
    inner = lax.slice_in_dim(forces, 1, size_dim - 1, axis=dim)
    lowest = [slice(None)] * inner.ndim
    lowest[dim] = 0
    highest = [slice(None)] * inner.ndim
    highest[dim] = size_dim - 3
    inner = inner.at[tuple(lowest)].add(lax.index_in_dim(arrived, 0, dim, keepdims=False))
    return inner.at[tuple(highest)].add(lax.index_in_dim(arrived, 3, dim, keepdims=False))


def per_device(positions, charges, atom_types, atom_counts, type_sigma, type_epsilon, pair_list):
    first_cells, second_cells, third_cells, slots = charges.shape
    live_slots = lax.broadcasted_iota(jnp.int32, charges.shape, 3) < atom_counts[..., None]
    charge_atom = jnp.where(live_slots, charges, 0.0)
    root_depth = jnp.sqrt(type_epsilon)
    sigma_atom, depth_atom = table_lookup(atom_types, live_slots, type_sigma, root_depth)
    local_atoms = jnp.concatenate([positions, jnp.stack([charge_atom, sigma_atom, depth_atom])], 0)
    extended = padded_2(local_atoms, (("gx", 1), ("gy", 2), ("gz", 3)), 1)
    span_second = second_cells + 2
    span_third = third_cells + 2
    ext_cells = (first_cells + 2) * span_second * span_third
    flat_atoms = extended.reshape(6, ext_cells, slots)
    cell_all = pair_list[0].reshape(-1)
    code_all = pair_list[1].reshape(-1)
    total_slots = cell_all.shape[0]
    padded = (total_slots + block_pairs - 1) // block_pairs * block_pairs
    cell_all = jnp.pad(cell_all, (0, padded - total_slots))
    code_all = jnp.pad(code_all, (0, padded - total_slots), constant_values=-1)

    def block_step(block_index, forces):
        first_slot = block_index * block_pairs
        cell_ids = lax.dynamic_slice_in_dim(cell_all, first_slot, block_pairs)
        code_ids = lax.dynamic_slice_in_dim(code_all, first_slot, block_pairs)
        move_first, move_second, move_third, weight = decode(code_ids)
        local_first = cell_ids // (second_cells * third_cells) + 1
        local_second = cell_ids // third_cells % second_cells + 1
        local_third = cell_ids % third_cells + 1
        home_cell = (local_first * span_second + local_second) * span_third + local_third
        other_cell = (
            ((local_first + move_first) * span_second + local_second + move_second) * span_third
            + local_third
            + move_third
        )
        left_atoms = jnp.take(flat_atoms, home_cell, axis=1)
        right_atoms = jnp.take(flat_atoms, other_cell, axis=1)
        offset = -cell_edge * jnp.stack([move_first, move_second, move_third]).astype(jnp.float32)
        on_left, on_right = pair_forces(left_atoms, right_atoms, offset)
        forces = forces.at[:, home_cell].add(on_left * weight[None, :, None])
        return forces.at[:, other_cell].add(on_right * weight[None, :, None])

    block_count = padded // block_pairs
    start_forces = jnp.zeros((3, ext_cells, slots), jnp.float32)
    forces = lax.fori_loop(0, block_count, block_step, start_forces)
    forces = forces.reshape(3, first_cells + 2, span_second, span_third, slots)
    axis_order = ("gx", "gy", "gz")
    for axis_name in axis_order:
        if axis_name == "gx":
            arrived_x = padded_2(edge_rims(forces, 1), (("gx", 1),), 1)
            forces = settle(forces, 1, arrived_x)
        elif axis_name == "gy":
            arrived_y = padded_2(edge_rims(forces, 2), (("gy", 2),), 1)
            forces = settle(forces, 2, arrived_y)
        else:
            arrived_z = padded_2(edge_rims(forces, 3), (("gz", 3),), 1)
            forces = settle(forces, 3, arrived_z)
    return forces


def solution(mesh):
    placed = (
        P(None, "gx", "gy", "gz", None),
        P("gx", "gy", "gz", None),
        P("gx", "gy", "gz", None),
        P("gx", "gy", "gz"),
        P(),
        P(),
        P(None, "gx", "gy", "gz", None),
    )
    return jax.shard_map(
        per_device,
        mesh=mesh,
        in_specs=placed,
        out_specs=P(None, "gx", "gy", "gz", None),
        check_vma=False,
    )
```

profile of v0, /device:TPU:1, one launch (start us, length us, event | category | flops | bytes accessed | tf_op | source)
XLA Modules:
  0.0 167.5 jit_solution(2258966891221933787)
XLA Ops:
  2.8 4.8 %collective-permute-start = (f32[6,1,2,2,128]{4,3,2,1,0:T(2,128)S(1)}, f32[6,1,2,2,128]{4,3,2,1,0:T(2,128)S(1)}, u32[]{:S(2)}, u32[]{:S(2)}) collective-permute-start(f32[6,1,2,2,128]{4,3,2,1,0:T(2,128)S(1)} %get-tuple-element.361), channel_id=1, source_target_pairs={{0,64},{64,128},{128,192},{192,256},{256,320},{320,384},{384,448},... | collective-permute-start | bytes 36872 | tf_op jit(solution)/shard_map/ppermute | solution.py:20
  7.6 15.9 %collective-permute-start.1 = (f32[6,1,2,2,128]{4,3,2,1,0:T(2,128)S(1)}, f32[6,1,2,2,128]{4,3,2,1,0:T(2,128)S(1)}, u32[]{:S(2)}, u32[]{:S(2)}) collective-permute-start(f32[6,1,2,2,128]{4,3,2,1,0:T(2,128)S(1)} %get-tuple-element.362), channel_id=1, source_target_pairs={{64,0},{128,64},{192,128},{256,192},{320,256},{384,320},{448,384},... | collective-permute-start | bytes 36872 | tf_op jit(solution)/shard_map/ppermute | solution.py:21
  24.4 2.7 %collective-permute-start.2 = (f32[6,4,1,2,128]{4,3,2,1,0:T(2,128)S(1)}, f32[6,4,1,2,128]{4,3,2,1,0:T(2,128)S(1)}, u32[]{:S(2)}, u32[]{:S(2)}) collective-permute-start(f32[6,4,1,2,128]{4,3,2,1,0:T(2,128)S(1)} %get-tuple-element.357), channel_id=1, source_target_pairs={{0,4},{4,8},{8,12},{12,16},{16,20},{20,24},{24,28},{28,32},{32,36}... | collective-permute-start | bytes 73736 | tf_op jit(solution)/shard_map/ppermute | solution.py:20
  27.1 0.9 collective-permute-done.2
  28.0 2.3 %collective-permute-done.3 = f32[6,4,1,2,128]{4,3,2,1,0:T(2,128)S(1)} collective-permute-done((f32[6,4,1,2,128]{4,3,2,1,0:T(2,128)S(1)}, f32[6,4,1,2,128]{4,3,2,1,0:T(2,128)S(1)}, u32[]{:S(2)}, u32[]{:S(2)}) %collective-permute-start.3) | collective-permute-done | bytes 24608 | tf_op jit(solution)/shard_map/ppermute | solution.py:21
  30.5 3.1 %collective-permute-start.4 = (f32[6,4,4,1,128]{4,3,2,1,0:T(1,128)S(1)}, f32[6,4,4,1,128]{4,3,2,1,0:T(1,128)S(1)}, u32[]{:S(2)}, u32[]{:S(2)}) collective-permute-start(f32[6,4,4,1,128]{4,3,2,1,0:T(1,128)S(1)} %get-tuple-element.353), channel_id=1, source_target_pairs={{0,1},{1,2},{2,3},{3,0},{4,5},{5,6},{6,7},{7,4},{8,9},{9,10},{10,1... | collective-permute-start | bytes 147464 | tf_op jit(solution)/shard_map/ppermute | solution.py:20
  33.6 3.4 %collective-permute-start.5 = (f32[6,4,4,1,128]{4,3,2,1,0:T(1,128)S(1)}, f32[6,4,4,1,128]{4,3,2,1,0:T(1,128)S(1)}, u32[]{:S(2)}, u32[]{:S(2)}) collective-permute-start(f32[6,4,4,1,128]{4,3,2,1,0:T(1,128)S(1)} %get-tuple-element.354), channel_id=1, source_target_pairs={{1,0},{2,1},{3,2},{0,3},{5,4},{6,5},{7,6},{4,7},{9,8},{10,9},{11,1... | collective-permute-start | bytes 147464 | tf_op jit(solution)/shard_map/ppermute | solution.py:21
  37.0 1.4 collective-permute-done.5
  38.7 105.9 %while.24 = (s32[]{:T(128)}, f32[3,64,128]{2,0,1:T(4,128)S(1)}, s32[192]{0:T(256)S(1)}, f32[6,64,128]{2,0,1:T(8,128)S(1)}, s32[192]{0:T(256)S(1)}, /*index=5*/s32[]{:T(128)}, s32[]{:T(128)}, s32[]{:T(128)}, s32[]{:T(128)}) while((s32[]{:T(128)}, f32[3,64,128]{2,0,1:T(4,128)S(1)}, s32[192]{0:T(256)S(1)}, f32[6,64,128]{2,0,1:T(8,128)S(1)}, ...), condition=%wide.region_11.13_spmd, body=%wide.region_2.12_spmd.sunk | while | flops 11459018 | bytes 968723 | solution.py:142
  40.5 2.7 %fusion.58 = (f32[12,128]{1,0:T(8,128)S(1)}, f32[12,128]{1,0:T(8,128)S(1)}, f32[12,128]{1,0:T(8,128)S(1)}, f32[12,128]{1,0:T(8,128)S(1)}, f32[12,128]{1,0:T(8,128)S(1)}, /*index=5*/f32[12,128]{1,0:T(8,128)S(1)}) fusion(f32[12]{0:T(128)S(1)} %get-tuple-element.451, f32[12,128]{1,0:T(8,128)S(1)} %get-tuple-element.456, ...), kind=kLoop, calls=%fused_computation.25.clone.1 | loop fusion | flops 11394048 | bytes 110736 | tf_op jit(solution)/shard_map/while/body/eval_jaxpr/reduce_sum | solution.py:78
  43.3 1.0 scatter_fusion
  44.3 1.0 scatter_fusion.1
  47.1 2.7 %fusion.58 = (f32[12,128]{1,0:T(8,128)S(1)}, f32[12,128]{1,0:T(8,128)S(1)}, f32[12,128]{1,0:T(8,128)S(1)}, f32[12,128]{1,0:T(8,128)S(1)}, f32[12,128]{1,0:T(8,128)S(1)}, /*index=5*/f32[12,128]{1,0:T(8,128)S(1)}) fusion(f32[12]{0:T(128)S(1)} %get-tuple-element.451, f32[12,128]{1,0:T(8,128)S(1)} %get-tuple-element.456, ...), kind=kLoop, calls=%fused_computation.25.clone.1 | loop fusion | flops 11394048 | bytes 110736 | tf_op jit(solution)/shard_map/while/body/eval_jaxpr/reduce_sum | solution.py:78
  49.9 1.0 scatter_fusion
  50.9 1.0 scatter_fusion.1
  53.7 2.7 %fusion.58 = (f32[12,128]{1,0:T(8,128)S(1)}, f32[12,128]{1,0:T(8,128)S(1)}, f32[12,128]{1,0:T(8,128)S(1)}, f32[12,128]{1,0:T(8,128)S(1)}, f32[12,128]{1,0:T(8,128)S(1)}, /*index=5*/f32[12,128]{1,0:T(8,128)S(1)}) fusion(f32[12]{0:T(128)S(1)} %get-tuple-element.451, f32[12,128]{1,0:T(8,128)S(1)} %get-tuple-element.456, ...), kind=kLoop, calls=%fused_computation.25.clone.1 | loop fusion | flops 11394048 | bytes 110736 | tf_op jit(solution)/shard_map/while/body/eval_jaxpr/reduce_sum | solution.py:78
  56.5 1.0 scatter_fusion
  57.5 1.0 scatter_fusion.1
  60.3 2.7 %fusion.58 = (f32[12,128]{1,0:T(8,128)S(1)}, f32[12,128]{1,0:T(8,128)S(1)}, f32[12,128]{1,0:T(8,128)S(1)}, f32[12,128]{1,0:T(8,128)S(1)}, f32[12,128]{1,0:T(8,128)S(1)}, /*index=5*/f32[12,128]{1,0:T(8,128)S(1)}) fusion(f32[12]{0:T(128)S(1)} %get-tuple-element.451, f32[12,128]{1,0:T(8,128)S(1)} %get-tuple-element.456, ...), kind=kLoop, calls=%fused_computation.25.clone.1 | loop fusion | flops 11394048 | bytes 110736 | tf_op jit(solution)/shard_map/while/body/eval_jaxpr/reduce_sum | solution.py:78
  63.1 1.0 scatter_fusion
  64.1 1.0 scatter_fusion.1
  66.9 2.7 %fusion.58 = (f32[12,128]{1,0:T(8,128)S(1)}, f32[12,128]{1,0:T(8,128)S(1)}, f32[12,128]{1,0:T(8,128)S(1)}, f32[12,128]{1,0:T(8,128)S(1)}, f32[12,128]{1,0:T(8,128)S(1)}, /*index=5*/f32[12,128]{1,0:T(8,128)S(1)}) fusion(f32[12]{0:T(128)S(1)} %get-tuple-element.451, f32[12,128]{1,0:T(8,128)S(1)} %get-tuple-element.456, ...), kind=kLoop, calls=%fused_computation.25.clone.1 | loop fusion | flops 11394048 | bytes 110736 | tf_op jit(solution)/shard_map/while/body/eval_jaxpr/reduce_sum | solution.py:78
  69.7 1.0 scatter_fusion
  70.7 1.0 scatter_fusion.1
  73.5 2.7 %fusion.58 = (f32[12,128]{1,0:T(8,128)S(1)}, f32[12,128]{1,0:T(8,128)S(1)}, f32[12,128]{1,0:T(8,128)S(1)}, f32[12,128]{1,0:T(8,128)S(1)}, f32[12,128]{1,0:T(8,128)S(1)}, /*index=5*/f32[12,128]{1,0:T(8,128)S(1)}) fusion(f32[12]{0:T(128)S(1)} %get-tuple-element.451, f32[12,128]{1,0:T(8,128)S(1)} %get-tuple-element.456, ...), kind=kLoop, calls=%fused_computation.25.clone.1 | loop fusion | flops 11394048 | bytes 110736 | tf_op jit(solution)/shard_map/while/body/eval_jaxpr/reduce_sum | solution.py:78
  76.3 1.0 scatter_fusion
  77.4 1.0 scatter_fusion.1
  80.1 2.7 %fusion.58 = (f32[12,128]{1,0:T(8,128)S(1)}, f32[12,128]{1,0:T(8,128)S(1)}, f32[12,128]{1,0:T(8,128)S(1)}, f32[12,128]{1,0:T(8,128)S(1)}, f32[12,128]{1,0:T(8,128)S(1)}, /*index=5*/f32[12,128]{1,0:T(8,128)S(1)}) fusion(f32[12]{0:T(128)S(1)} %get-tuple-element.451, f32[12,128]{1,0:T(8,128)S(1)} %get-tuple-element.456, ...), kind=kLoop, calls=%fused_computation.25.clone.1 | loop fusion | flops 11394048 | bytes 110736 | tf_op jit(solution)/shard_map/while/body/eval_jaxpr/reduce_sum | solution.py:78
  82.9 1.0 scatter_fusion
  84.0 1.0 scatter_fusion.1
  86.7 2.7 %fusion.58 = (f32[12,128]{1,0:T(8,128)S(1)}, f32[12,128]{1,0:T(8,128)S(1)}, f32[12,128]{1,0:T(8,128)S(1)}, f32[12,128]{1,0:T(8,128)S(1)}, f32[12,128]{1,0:T(8,128)S(1)}, /*index=5*/f32[12,128]{1,0:T(8,128)S(1)}) fusion(f32[12]{0:T(128)S(1)} %get-tuple-element.451, f32[12,128]{1,0:T(8,128)S(1)} %get-tuple-element.456, ...), kind=kLoop, calls=%fused_computation.25.clone.1 | loop fusion | flops 11394048 | bytes 110736 | tf_op jit(solution)/shard_map/while/body/eval_jaxpr/reduce_sum | solution.py:78
  89.5 1.0 scatter_fusion
  90.6 1.0 scatter_fusion.1
  93.4 2.7 %fusion.58 = (f32[12,128]{1,0:T(8,128)S(1)}, f32[12,128]{1,0:T(8,128)S(1)}, f32[12,128]{1,0:T(8,128)S(1)}, f32[12,128]{1,0:T(8,128)S(1)}, f32[12,128]{1,0:T(8,128)S(1)}, /*index=5*/f32[12,128]{1,0:T(8,128)S(1)}) fusion(f32[12]{0:T(128)S(1)} %get-tuple-element.451, f32[12,128]{1,0:T(8,128)S(1)} %get-tuple-element.456, ...), kind=kLoop, calls=%fused_computation.25.clone.1 | loop fusion | flops 11394048 | bytes 110736 | tf_op jit(solution)/shard_map/while/body/eval_jaxpr/reduce_sum | solution.py:78
  96.2 1.0 scatter_fusion
  97.2 1.0 scatter_fusion.1
  100.0 2.7 %fusion.58 = (f32[12,128]{1,0:T(8,128)S(1)}, f32[12,128]{1,0:T(8,128)S(1)}, f32[12,128]{1,0:T(8,128)S(1)}, f32[12,128]{1,0:T(8,128)S(1)}, f32[12,128]{1,0:T(8,128)S(1)}, /*index=5*/f32[12,128]{1,0:T(8,128)S(1)}) fusion(f32[12]{0:T(128)S(1)} %get-tuple-element.451, f32[12,128]{1,0:T(8,128)S(1)} %get-tuple-element.456, ...), kind=kLoop, calls=%fused_computation.25.clone.1 | loop fusion | flops 11394048 | bytes 110736 | tf_op jit(solution)/shard_map/while/body/eval_jaxpr/reduce_sum | solution.py:78
  102.8 1.0 scatter_fusion
  103.8 1.0 scatter_fusion.1
  106.6 2.7 %fusion.58 = (f32[12,128]{1,0:T(8,128)S(1)}, f32[12,128]{1,0:T(8,128)S(1)}, f32[12,128]{1,0:T(8,128)S(1)}, f32[12,128]{1,0:T(8,128)S(1)}, f32[12,128]{1,0:T(8,128)S(1)}, /*index=5*/f32[12,128]{1,0:T(8,128)S(1)}) fusion(f32[12]{0:T(128)S(1)} %get-tuple-element.451, f32[12,128]{1,0:T(8,128)S(1)} %get-tuple-element.456, ...), kind=kLoop, calls=%fused_computation.25.clone.1 | loop fusion | flops 11394048 | bytes 110736 | tf_op jit(solution)/shard_map/while/body/eval_jaxpr/reduce_sum | solution.py:78
  109.4 1.0 scatter_fusion
  110.5 1.0 scatter_fusion.1
  113.3 2.7 %fusion.58 = (f32[12,128]{1,0:T(8,128)S(1)}, f32[12,128]{1,0:T(8,128)S(1)}, f32[12,128]{1,0:T(8,128)S(1)}, f32[12,128]{1,0:T(8,128)S(1)}, f32[12,128]{1,0:T(8,128)S(1)}, /*index=5*/f32[12,128]{1,0:T(8,128)S(1)}) fusion(f32[12]{0:T(128)S(1)} %get-tuple-element.451, f32[12,128]{1,0:T(8,128)S(1)} %get-tuple-element.456, ...), kind=kLoop, calls=%fused_computation.25.clone.1 | loop fusion | flops 11394048 | bytes 110736 | tf_op jit(solution)/shard_map/while/body/eval_jaxpr/reduce_sum | solution.py:78
  116.1 1.0 scatter_fusion
  117.1 1.0 scatter_fusion.1
  119.9 2.7 %fusion.58 = (f32[12,128]{1,0:T(8,128)S(1)}, f32[12,128]{1,0:T(8,128)S(1)}, f32[12,128]{1,0:T(8,128)S(1)}, f32[12,128]{1,0:T(8,128)S(1)}, f32[12,128]{1,0:T(8,128)S(1)}, /*index=5*/f32[12,128]{1,0:T(8,128)S(1)}) fusion(f32[12]{0:T(128)S(1)} %get-tuple-element.451, f32[12,128]{1,0:T(8,128)S(1)} %get-tuple-element.456, ...), kind=kLoop, calls=%fused_computation.25.clone.1 | loop fusion | flops 11394048 | bytes 110736 | tf_op jit(solution)/shard_map/while/body/eval_jaxpr/reduce_sum | solution.py:78
  122.7 1.0 scatter_fusion
  123.7 1.0 scatter_fusion.1
  126.5 2.7 %fusion.58 = (f32[12,128]{1,0:T(8,128)S(1)}, f32[12,128]{1,0:T(8,128)S(1)}, f32[12,128]{1,0:T(8,128)S(1)}, f32[12,128]{1,0:T(8,128)S(1)}, f32[12,128]{1,0:T(8,128)S(1)}, /*index=5*/f32[12,128]{1,0:T(8,128)S(1)}) fusion(f32[12]{0:T(128)S(1)} %get-tuple-element.451, f32[12,128]{1,0:T(8,128)S(1)} %get-tuple-element.456, ...), kind=kLoop, calls=%fused_computation.25.clone.1 | loop fusion | flops 11394048 | bytes 110736 | tf_op jit(solution)/shard_map/while/body/eval_jaxpr/reduce_sum | solution.py:78
  129.3 1.0 scatter_fusion
  130.3 1.0 scatter_fusion.1
  133.1 2.7 %fusion.58 = (f32[12,128]{1,0:T(8,128)S(1)}, f32[12,128]{1,0:T(8,128)S(1)}, f32[12,128]{1,0:T(8,128)S(1)}, f32[12,128]{1,0:T(8,128)S(1)}, f32[12,128]{1,0:T(8,128)S(1)}, /*index=5*/f32[12,128]{1,0:T(8,128)S(1)}) fusion(f32[12]{0:T(128)S(1)} %get-tuple-element.451, f32[12,128]{1,0:T(8,128)S(1)} %get-tuple-element.456, ...), kind=kLoop, calls=%fused_computation.25.clone.1 | loop fusion | flops 11394048 | bytes 110736 | tf_op jit(solution)/shard_map/while/body/eval_jaxpr/reduce_sum | solution.py:78
  135.9 1.0 scatter_fusion
  137.0 1.0 scatter_fusion.1
  139.8 2.7 %fusion.58 = (f32[12,128]{1,0:T(8,128)S(1)}, f32[12,128]{1,0:T(8,128)S(1)}, f32[12,128]{1,0:T(8,128)S(1)}, f32[12,128]{1,0:T(8,128)S(1)}, f32[12,128]{1,0:T(8,128)S(1)}, /*index=5*/f32[12,128]{1,0:T(8,128)S(1)}) fusion(f32[12]{0:T(128)S(1)} %get-tuple-element.451, f32[12,128]{1,0:T(8,128)S(1)} %get-tuple-element.456, ...), kind=kLoop, calls=%fused_computation.25.clone.1 | loop fusion | flops 11394048 | bytes 110736 | tf_op jit(solution)/shard_map/while/body/eval_jaxpr/reduce_sum | solution.py:78
  142.6 1.0 scatter_fusion
  143.6 1.0 scatter_fusion.1
  144.7 1.9 %collective-permute-start.6 = (f32[3,1,4,4,128]{4,3,2,1,0:T(4,128)S(1)}, f32[3,1,4,4,128]{4,3,2,1,0:T(4,128)S(1)}, u32[]{:S(2)}, u32[]{:S(2)}) collective-permute-start(f32[3,1,4,4,128]{4,3,2,1,0:T(4,128)S(1)} %get-tuple-element.352), channel_id=1, source_target_pairs={{0,64},{64,128},{128,192},{192,256},{256,320},{320,384},{384,448},... | collective-permute-start | bytes 73736 | tf_op jit(solution)/shard_map/ppermute | solution.py:20
  146.6 5.1 %collective-permute-start.7 = (f32[3,1,4,4,128]{4,3,2,1,0:T(4,128)S(1)}, f32[3,1,4,4,128]{4,3,2,1,0:T(4,128)S(1)}, u32[]{:S(2)}, u32[]{:S(2)}) collective-permute-start(f32[3,1,4,4,128]{4,3,2,1,0:T(4,128)S(1)} %get-tuple-element.351), channel_id=1, source_target_pairs={{64,0},{128,64},{192,128},{256,192},{320,256},{384,320},{448,384},... | collective-permute-start | bytes 73736 | tf_op jit(solution)/shard_map/ppermute | solution.py:21
  152.7 2.4 %collective-permute-start.8 = (f32[3,2,1,4,128]{4,3,2,1,0:T(4,128)S(1)}, f32[3,2,1,4,128]{4,3,2,1,0:T(4,128)S(1)}, u32[]{:S(2)}, u32[]{:S(2)}) collective-permute-start(f32[3,2,1,4,128]{4,3,2,1,0:T(4,128)S(1)} %get-tuple-element.356), channel_id=1, source_target_pairs={{0,4},{4,8},{8,12},{12,16},{16,20},{20,24},{24,28},{28,32},{32,36}... | collective-permute-start | bytes 36872 | tf_op jit(solution)/shard_map/ppermute | solution.py:20
  156.0 2.6 %collective-permute-done.9 = f32[3,2,1,4,128]{4,3,2,1,0:T(4,128)S(1)} collective-permute-done((f32[3,2,1,4,128]{4,3,2,1,0:T(4,128)S(1)}, f32[3,2,1,4,128]{4,3,2,1,0:T(4,128)S(1)}, u32[]{:S(2)}, u32[]{:S(2)}) %collective-permute-start.9) | collective-permute-done | bytes 12320 | tf_op jit(solution)/shard_map/ppermute | solution.py:21
  158.6 3.1 %collective-permute-start.10 = (f32[3,2,2,1,128]{4,3,2,1,0:T(1,128)S(1)}, f32[3,2,2,1,128]{4,3,2,1,0:T(1,128)S(1)}, u32[]{:S(2)}, u32[]{:S(2)}) collective-permute-start(f32[3,2,2,1,128]{4,3,2,1,0:T(1,128)S(1)} %get-tuple-element.360), channel_id=1, source_target_pairs={{0,1},{1,2},{2,3},{3,0},{4,5},{5,6},{6,7},{7,4},{8,9},{9,10},{10,1... | collective-permute-start | bytes 18440 | tf_op jit(solution)/shard_map/ppermute | solution.py:20
  161.7 3.4 %collective-permute-start.11 = (f32[3,2,2,1,128]{4,3,2,1,0:T(1,128)S(1)}, f32[3,2,2,1,128]{4,3,2,1,0:T(1,128)S(1)}, u32[]{:S(2)}, u32[]{:S(2)}) collective-permute-start(f32[3,2,2,1,128]{4,3,2,1,0:T(1,128)S(1)} %get-tuple-element.359), channel_id=1, source_target_pairs={{1,0},{2,1},{3,2},{0,3},{5,4},{6,5},{7,6},{4,7},{9,8},{10,9},{11,1... | collective-permute-start | bytes 18440 | tf_op jit(solution)/shard_map/ppermute | solution.py:21
  166.1 1.3 scatter-add.71
  (420 shorter events, 34.2 us)
Async XLA Ops:
  0.7 0.8 copy-start.3
  0.7 0.8 copy-start.5
  2.0 0.7 copy-start.2
  2.0 0.8 copy-start
  2.8 20.7 %collective-permute-start = (f32[6,1,2,2,128]{4,3,2,1,0:T(2,128)S(1)}, f32[6,1,2,2,128]{4,3,2,1,0:T(2,128)S(1)}, u32[]{:S(2)}, u32[]{:S(2)}) collective-permute-start(f32[6,1,2,2,128]{4,3,2,1,0:T(2,128)S(1)} %get-tuple-element.361), channel_id=1, source_target_pairs={{0,64},{64,128},{128,192},{192,256},{256,320},{320,384},{384,448},... | collective-permute-start | bytes 36872 | tf_op jit(solution)/shard_map/ppermute | solution.py:20
  7.6 16.7 %collective-permute-start.1 = (f32[6,1,2,2,128]{4,3,2,1,0:T(2,128)S(1)}, f32[6,1,2,2,128]{4,3,2,1,0:T(2,128)S(1)}, u32[]{:S(2)}, u32[]{:S(2)}) collective-permute-start(f32[6,1,2,2,128]{4,3,2,1,0:T(2,128)S(1)} %get-tuple-element.362), channel_id=1, source_target_pairs={{64,0},{128,64},{192,128},{256,192},{320,256},{384,320},{448,384},... | collective-permute-start | bytes 36872 | tf_op jit(solution)/shard_map/ppermute | solution.py:21
  24.4 3.7 %collective-permute-start.2 = (f32[6,4,1,2,128]{4,3,2,1,0:T(2,128)S(1)}, f32[6,4,1,2,128]{4,3,2,1,0:T(2,128)S(1)}, u32[]{:S(2)}, u32[]{:S(2)}) collective-permute-start(f32[6,4,1,2,128]{4,3,2,1,0:T(2,128)S(1)} %get-tuple-element.357), channel_id=1, source_target_pairs={{0,4},{4,8},{8,12},{12,16},{16,20},{20,24},{24,28},{28,32},{32,36}... | collective-permute-start | bytes 73736 | tf_op jit(solution)/shard_map/ppermute | solution.py:20
  27.1 3.3 %collective-permute-start.3 = (f32[6,4,1,2,128]{4,3,2,1,0:T(2,128)S(1)}, f32[6,4,1,2,128]{4,3,2,1,0:T(2,128)S(1)}, u32[]{:S(2)}, u32[]{:S(2)}) collective-permute-start(f32[6,4,1,2,128]{4,3,2,1,0:T(2,128)S(1)} %get-tuple-element.358), channel_id=1, source_target_pairs={{4,0},{8,4},{12,8},{16,12},{20,16},{24,20},{28,24},{32,28},{36,32}... | collective-permute-start | bytes 73736 | tf_op jit(solution)/shard_map/ppermute | solution.py:21
  30.5 6.5 %copy-start.4 = (s32[2,1,1,1,188]{4,3,2,1,0:T(1,128)S(1)}, s32[2,1,1,1,188]{4,3,2,1,0:T(1,128)}, u32[]{:S(2)}) copy-start(s32[2,1,1,1,188]{4,3,2,1,0:T(1,128)} %param.29) | copy-start | bytes 4516
  30.5 6.6 %collective-permute-start.4 = (f32[6,4,4,1,128]{4,3,2,1,0:T(1,128)S(1)}, f32[6,4,4,1,128]{4,3,2,1,0:T(1,128)S(1)}, u32[]{:S(2)}, u32[]{:S(2)}) collective-permute-start(f32[6,4,4,1,128]{4,3,2,1,0:T(1,128)S(1)} %get-tuple-element.353), channel_id=1, source_target_pairs={{0,1},{1,2},{2,3},{3,0},{4,5},{5,6},{6,7},{7,4},{8,9},{9,10},{10,1... | collective-permute-start | bytes 147464 | tf_op jit(solution)/shard_map/ppermute | solution.py:20
  33.6 4.8 %collective-permute-start.5 = (f32[6,4,4,1,128]{4,3,2,1,0:T(1,128)S(1)}, f32[6,4,4,1,128]{4,3,2,1,0:T(1,128)S(1)}, u32[]{:S(2)}, u32[]{:S(2)}) collective-permute-start(f32[6,4,4,1,128]{4,3,2,1,0:T(1,128)S(1)} %get-tuple-element.354), channel_id=1, source_target_pairs={{1,0},{2,1},{3,2},{0,3},{5,4},{6,5},{7,6},{4,7},{9,8},{10,9},{11,1... | collective-permute-start | bytes 147464 | tf_op jit(solution)/shard_map/ppermute | solution.py:21
  144.7 7.1 %collective-permute-start.6 = (f32[3,1,4,4,128]{4,3,2,1,0:T(4,128)S(1)}, f32[3,1,4,4,128]{4,3,2,1,0:T(4,128)S(1)}, u32[]{:S(2)}, u32[]{:S(2)}) collective-permute-start(f32[3,1,4,4,128]{4,3,2,1,0:T(4,128)S(1)} %get-tuple-element.352), channel_id=1, source_target_pairs={{0,64},{64,128},{128,192},{192,256},{256,320},{320,384},{384,448},... | collective-permute-start | bytes 73736 | tf_op jit(solution)/shard_map/ppermute | solution.py:20
  146.6 6.1 %collective-permute-start.7 = (f32[3,1,4,4,128]{4,3,2,1,0:T(4,128)S(1)}, f32[3,1,4,4,128]{4,3,2,1,0:T(4,128)S(1)}, u32[]{:S(2)}, u32[]{:S(2)}) collective-permute-start(f32[3,1,4,4,128]{4,3,2,1,0:T(4,128)S(1)} %get-tuple-element.351), channel_id=1, source_target_pairs={{64,0},{128,64},{192,128},{256,192},{320,256},{384,320},{448,384},... | collective-permute-start | bytes 73736 | tf_op jit(solution)/shard_map/ppermute | solution.py:21
  152.7 3.2 %collective-permute-start.8 = (f32[3,2,1,4,128]{4,3,2,1,0:T(4,128)S(1)}, f32[3,2,1,4,128]{4,3,2,1,0:T(4,128)S(1)}, u32[]{:S(2)}, u32[]{:S(2)}) collective-permute-start(f32[3,2,1,4,128]{4,3,2,1,0:T(4,128)S(1)} %get-tuple-element.356), channel_id=1, source_target_pairs={{0,4},{4,8},{8,12},{12,16},{16,20},{20,24},{24,28},{28,32},{32,36}... | collective-permute-start | bytes 36872 | tf_op jit(solution)/shard_map/ppermute | solution.py:20
  155.1 3.4 %collective-permute-start.9 = (f32[3,2,1,4,128]{4,3,2,1,0:T(4,128)S(1)}, f32[3,2,1,4,128]{4,3,2,1,0:T(4,128)S(1)}, u32[]{:S(2)}, u32[]{:S(2)}) collective-permute-start(f32[3,2,1,4,128]{4,3,2,1,0:T(4,128)S(1)} %get-tuple-element.355), channel_id=1, source_target_pairs={{4,0},{8,4},{12,8},{16,12},{20,16},{24,20},{28,24},{32,28},{36,32}... | collective-permute-start | bytes 36872 | tf_op jit(solution)/shard_map/ppermute | solution.py:21
  158.6 6.5 %collective-permute-start.10 = (f32[3,2,2,1,128]{4,3,2,1,0:T(1,128)S(1)}, f32[3,2,2,1,128]{4,3,2,1,0:T(1,128)S(1)}, u32[]{:S(2)}, u32[]{:S(2)}) collective-permute-start(f32[3,2,2,1,128]{4,3,2,1,0:T(1,128)S(1)} %get-tuple-element.360), channel_id=1, source_target_pairs={{0,1},{1,2},{2,3},{3,0},{4,5},{5,6},{6,7},{7,4},{8,9},{9,10},{10,1... | collective-permute-start | bytes 18440 | tf_op jit(solution)/shard_map/ppermute | solution.py:20
  161.7 4.4 %collective-permute-start.11 = (f32[3,2,2,1,128]{4,3,2,1,0:T(1,128)S(1)}, f32[3,2,2,1,128]{4,3,2,1,0:T(1,128)S(1)}, u32[]{:S(2)}, u32[]{:S(2)}) collective-permute-start(f32[3,2,2,1,128]{4,3,2,1,0:T(1,128)S(1)} %get-tuple-element.359), channel_id=1, source_target_pairs={{1,0},{2,1},{3,2},{0,3},{5,4},{6,5},{7,6},{4,7},{9,8},{10,9},{11,1... | collective-permute-start | bytes 18440 | tf_op jit(solution)/shard_map/ppermute | solution.py:21
  165.2 0.9 copy-start.1
where the time goes:
time: 171 us; the launch traced here: 167 us
  other arithmetic  85.6 us (50%)
  starting transfers between devices  45.9 us (27%)
  local copies, waits for them, and re-layouts  22.2 us (13%)
  waiting for transfers between devices  10.6 us (6%)
  loops' own time  2.85 us (2%)
    reduce_sum x16, other arithmetic, pair_forces(): jnp.sum(pair_scale * component, 1)  42.9 us
    ppermute x6, starting transfers between devices, padded_2(): after = lax.ppermute(leading, axis, down)  27.7 us
    ppermute x6, starting transfers between devices, padded_2(): before = lax.ppermute(last, axis, up)  18.1 us
    scatter-add x16, other arithmetic, block_step(): forces = forces.at[:, home_cell].add(on_left * weight[None, :, None])  16.4 us
    scatter-add x16, other arithmetic, block_step(): return forces.at[:, other_cell].add(on_right * weight[None, :, None])  16.3 us
    gather x16, local copies, waits for them, and re-layouts, block_step(): left_atoms = jnp.take(flat_atoms, home_cell, axis=1)  8.94 us
    gather x16, local copies, waits for them, and re-layouts, block_step(): right_atoms = jnp.take(flat_atoms, other_cell, axis=1)  8.94 us
    ppermute x6, waiting for transfers between devices, padded_2(): after = lax.ppermute(leading, axis, down)  8.86 us
  transfers between devices with their start and end apart: 12, of which 8 were waited for; matrix products, arithmetic and copies ran while one was open for 0% of the time, Pallas kernels for 0%

commit v1 on v0

v1 whole, which is shorter than its diff:
```python
import math

import jax
import jax.numpy as jnp
from jax import lax
from jax.experimental import pallas as pl
from jax.experimental.pallas import tpu as pltpu
from jax.sharding import PartitionSpec as P

AXES = ("gx", "gy", "gz")
CUT = 144.0
WIDTH = 44.0
UNIT = 1.0 / math.sqrt(WIDTH)
EDGE = 12.0 * UNIT
CHARGE_UNIT = WIDTH ** -0.25
DEPTH_UNIT = math.sqrt(24.0)
FORCE_UNIT = 2.0 / WIDTH * math.sqrt(WIDTH)
COUNT_LANE = 27
META_ROW = 6
RELATIONS = [(r // 4, r // 2 % 2, r % 2) for r in range(1, 8)]
MAX_CHUNKS = 30


def parities():
    return [lax.rem(lax.axis_index(name), 2) for name in AXES]


def free_cells(relation, fixed, choices):
    spans = [[fixed[a]] if relation[a] else list(range(choices)) for a in range(3)]
    return [(x, y, z) for x in spans[0] for y in spans[1] for z in spans[2]]


def atoms_kernel(pos_ref, charge_ref, type_ref, count_ref, sigma_ref, eps_ref, pair_ref, own_ref, send_ref, rows_ref, kinds_ref, codes_ref):
    for i in range(2):
        for j in range(2):
            at = pl.ds(4 * i + 2 * j, 2)
            for comp in range(3):
                rows_ref[comp, at, :] = pos_ref[comp, i, j]
            rows_ref[3, at, :] = charge_ref[i, j]
            kinds_ref[at, :] = type_ref[i, j]
    codes_ref[...] = jnp.full(codes_ref.shape, -1, jnp.int32)
    slots = pair_ref.shape[-1]
    codes_ref[0:1, 0:slots] = pair_ref[0, 0, 0]
    codes_ref[1:2, 0:slots] = pair_ref[1, 0, 0]

    cell = lax.broadcasted_iota(jnp.int32, (8, 128), 0)
    lane = lax.broadcasted_iota(jnp.int32, (8, 128), 1)
    count = jnp.zeros((8, 128), jnp.int32)
    for c in range(8):
        count = jnp.where(cell == c, count_ref[c // 4, c // 2 % 2, c % 2], count)
    live = lane < count
    kinds = kinds_ref[...]
    sigma = jnp.broadcast_to(sigma_ref[...] * (0.5 * UNIT), (8, 128))
    depth = jnp.broadcast_to(jnp.sqrt(eps_ref[...]) * DEPTH_UNIT, (8, 128))
    sigma = jnp.take_along_axis(sigma, kinds, axis=1, mode="promise_in_bounds")
    depth = jnp.take_along_axis(depth, kinds, axis=1, mode="promise_in_bounds")

    cells = codes_ref[0:1, :]
    codes = codes_ref[1:2, :]
    width = codes_ref.shape[1]
    is_cell = lax.broadcasted_iota(jnp.int32, (8, width), 0) == cells
    is_code = lax.broadcasted_iota(jnp.int32, (128, width), 0) == codes
    listed = lax.dot_general(
        jnp.where(is_cell, 1.0, 0.0).astype(jnp.bfloat16),
        jnp.where(is_code, 1.0, 0.0).astype(jnp.bfloat16),
        (((1,), (1,)), ((), ())),
        preferred_element_type=jnp.float32,
    )
    meta = jnp.where(lane == COUNT_LANE, count.astype(jnp.float32), listed)

    values = [rows_ref[0] * UNIT, rows_ref[1] * UNIT, rows_ref[2] * UNIT]
    values.append(jnp.where(live, rows_ref[3] * CHARGE_UNIT, 0.0))
    values.append(jnp.where(live, sigma, 0.5 * UNIT))
    values.append(jnp.where(live, depth, 0.0))
    values += [meta, jnp.zeros((8, 128), jnp.float32)]
    for r in range(8):
        own_ref[:, r, :] = values[r]

    odd = parities()
    toward = [1 - b for b in odd]
    for rel in RELATIONS:
        slot = sum(lax.bitwise_xor(odd[a], rel[a]) * (4, 2, 1)[a] for a in range(3))
        for n, (x, y, z) in enumerate(free_cells(rel, toward, 2)):
            send_ref[slot, n] = own_ref[4 * x + 2 * y + z]


def relay_kernel(own_ref, got_ref, send_ref):
    odd = parities()
    for rel in RELATIONS:
        slot = sum(lax.bitwise_xor(1 - odd[a], rel[a]) * (4, 2, 1)[a] for a in range(3))
        for n, at in enumerate(free_cells(rel, odd, 3)):
            far = [isinstance(p, int) and p == 2 for p in at]
            if not any(far):
                send_ref[slot, n] = own_ref[4 * at[0] + 2 * at[1] + at[2]]
                continue
            source = sum(lax.bitwise_xor(odd[a], int(far[a])) * (4, 2, 1)[a] for a in range(3))
            m = 0
            for a in range(3):
                if not far[a]:
                    m = m * 2 + at[a]
            send_ref[slot, n] = got_ref[source, m]


def place(ext_ref, meta_ref, own_ref, even_ref, odd_ref):
    odd = parities()
    spot = [[1, 2, 3 - 3 * odd[a], 3 * odd[a]] for a in range(3)]

    def put(at, tile):
        where = spot[0][at[0]] * 16 + spot[1][at[1]] * 4 + spot[2][at[2]]
        ext_ref[where] = tile
        meta_ref[pl.ds(where, 1), :] = tile[META_ROW:META_ROW + 1, :].astype(jnp.int32)

    for c in range(8):
        put((c // 4, c // 2 % 2, c % 2), own_ref[c])
    for rel in RELATIONS:
        slot = sum(lax.bitwise_xor(odd[a], rel[a]) * (4, 2, 1)[a] for a in range(3))
        for n, at in enumerate(free_cells(rel, (2, 2, 2), 2)):
            put(at, even_ref[slot, n])
        slot = sum(lax.bitwise_xor(1 - odd[a], rel[a]) * (4, 2, 1)[a] for a in range(3))
        for n, at in enumerate(free_cells(rel, (3, 3, 3), 3)):
            put(at, odd_ref[slot, n])


def pair_terms(home, other):
    dx = home[0] - other[0]
    dy = home[1] - other[1]
    dz = home[2] - other[2]
    dist = dx * dx + dy * dy + dz * dz
    size = home[4] + other[4]
    size = size * size
    root = lax.rsqrt(dist + size)
    inverse = root * root
    ratio = size * inverse
    cube = ratio * ratio * ratio
    coulomb = home[3] * other[3] * root
    attract = home[5] * other[5] * cube
    repel = attract * cube
    core = repel - attract
    energy = core + 6.0 * coulomb
    slope = core + repel + coulomb
    inner = jnp.clip(CUT / WIDTH - dist, 0.0, 1.0)
    scale = inner * ((1.0 - inner) * energy + (inner * (1.5 - inner)) * inverse * slope)
    return scale * dx, scale * dy, scale * dz


def force_kernel(own_ref, even_ref, odd_ref, out_ref, ext_ref, meta_ref, info_ref, list_ref, cols_ref, sums_ref, rows_ref, sem):
    place(ext_ref, meta_ref, own_ref, even_ref, odd_ref)
    copy = pltpu.make_async_copy(meta_ref, info_ref, sem)
    copy.start()
    copy.wait()
    lane = lax.broadcasted_iota(jnp.int32, (8, 128), 1)
    row = lax.broadcasted_iota(jnp.int32, (8, 128), 0)
    filler = jnp.where(row < 3, 100.0, jnp.where(row == 4, 0.5 * UNIT, 0.0))

    def shift(move):
        vector = jnp.zeros((8, 128), jnp.float32)
        for a in range(3):
            if move[a]:
                vector = jnp.where(row == a, move[a] * EDGE, vector)
        return vector

    def cell_step(c, carry):
        here = (1 + c // 4) * 16 + (1 + c // 2 % 2) * 4 + 1 + c % 2
        atoms = info_ref[here, COUNT_LANE]
        end = jnp.int32(0)
        current = filler
        for code in range(27):
            move = (code // 9 - 1, code // 3 % 3 - 1, code % 3 - 1)
            there = here + move[0] * 16 + move[1] * 4 + move[2]
            listed = info_ref[here, code] + info_ref[there, 26 - code]
            size = jnp.where(listed > 0, info_ref[there, COUNT_LANE], 0)
            chunk = lax.shift_right_logical(end, 7)
            first = lax.bitwise_and(end, 127)
            tile = pltpu.roll(ext_ref[there] + shift(move), first, axis=1)
            merged = jnp.where(lane < first, current, tile)
            list_ref[chunk] = merged
            end = end + size
            current = jnp.where(lax.shift_right_logical(end, 7) > chunk, tile, merged)
        chunk = lax.shift_right_logical(end, 7)
        list_ref[chunk] = jnp.where(lane < lax.bitwise_and(end, 127), current, filler)
        list_ref[chunk + 1] = filler
        rounds = lax.shift_right_logical(end + 255, 8)
        cols_ref[...] = jnp.transpose(ext_ref[here])
        sums_ref[...] = jnp.zeros(sums_ref.shape, jnp.float32)

        def group_step(g, carry):
            first = pl.multiple_of(g * 16, 16)
            homes = []
            for h in range(2):
                cols = cols_ref[pl.ds(first + 8 * h, 8), :]
                homes.append([jnp.broadcast_to(cols[:, r:r + 1], (8, 128)) for r in range(6)])

            def chunk_step(k, sums):
                sums = list(sums)
                for u in range(2):
                    other = [jnp.broadcast_to(list_ref[2 * k + u, r:r + 1, :], (8, 128)) for r in range(6)]
                    for h in range(2):
                        terms = pair_terms(homes[h], other)
                        for a in range(3):
                            sums[3 * h + a] = sums[3 * h + a] + terms[a]
                return tuple(sums)

            sums = lax.fori_loop(0, rounds, chunk_step, (jnp.zeros((8, 128), jnp.float32),) * 6)
            for h in range(2):
                total = [jnp.sum(sums[3 * h + a], axis=1, keepdims=True) for a in range(3)]
                line = jnp.where(lane == 0, total[0], jnp.where(lane == 1, total[1], total[2]))
                sums_ref[pl.ds(first + 8 * h, 8), :] = line[:, 0:8]
            return carry

        lax.fori_loop(0, lax.shift_right_logical(atoms + 15, 4), group_step, 0)
        rows_ref[c] = jnp.transpose(sums_ref[...]) * FORCE_UNIT
        return carry

    lax.fori_loop(0, 8, cell_step, 0)
    for c in range(8):
        for a in range(3):
            out_ref[a, c // 4, c // 2 % 2, c % 2:c % 2 + 1, :] = rows_ref[c, a:a + 1, :]


def swap_groups(sizes, start):
    def index(x, y, z):
        return ((x % sizes[0]) * sizes[1] + y % sizes[1]) * sizes[2] + z % sizes[2]

    bits = [(b // 4, b // 2 % 2, b % 2) for b in range(8)]
    return [
        [index(x + start + bx, y + start + by, z + start + bz) for bx, by, bz in bits]
        for x in range(0, sizes[0], 2)
        for y in range(0, sizes[1], 2)
        for z in range(0, sizes[2], 2)
    ]


def per_device(positions, charges, atom_types, atom_counts, type_sigma, type_epsilon, pair_list):
    f32 = jnp.float32
    sizes = [lax.axis_size(name) for name in AXES]
    vmem = pl.BlockSpec(memory_space=pltpu.VMEM)
    smem = pl.BlockSpec(memory_space=pltpu.SMEM)
    own, send = pl.pallas_call(
        atoms_kernel,
        out_shape=(jax.ShapeDtypeStruct((8, 8, 128), f32), jax.ShapeDtypeStruct((8, 4, 8, 128), f32)),
        in_specs=[vmem, vmem, vmem, smem, vmem, vmem, vmem],
        out_specs=(vmem, vmem),
        scratch_shapes=[pltpu.VMEM((4, 8, 128), f32), pltpu.VMEM((8, 128), jnp.int32), pltpu.VMEM((8, 256), jnp.int32)],
        name="atoms",
    )(positions, charges, atom_types, atom_counts, type_sigma.reshape(1, -1), type_epsilon.reshape(1, -1), pair_list)
    even = lax.all_to_all(send, AXES, 0, 0, axis_index_groups=swap_groups(sizes, 0), tiled=True)
    send = pl.pallas_call(
        relay_kernel,
        out_shape=jax.ShapeDtypeStruct((8, 9, 8, 128), f32),
        in_specs=[vmem, vmem],
        out_specs=vmem,
        name="relay",
    )(own, even)
    odd = lax.all_to_all(send, AXES, 0, 0, axis_index_groups=swap_groups(sizes, 1), tiled=True)
    return pl.pallas_call(
        force_kernel,
        out_shape=jax.ShapeDtypeStruct((3, 2, 2, 2, 128), f32),
        in_specs=[vmem, vmem, vmem],
        out_specs=vmem,
        scratch_shapes=[
            pltpu.VMEM((64, 8, 128), f32),
            pltpu.VMEM((64, 128), jnp.int32),
            pltpu.SMEM((64, 128), jnp.int32),
            pltpu.VMEM((MAX_CHUNKS, 8, 128), f32),
            pltpu.VMEM((128, 8), f32),
            pltpu.VMEM((128, 8), f32),
            pltpu.VMEM((8, 8, 128), f32),
            pltpu.SemaphoreType.DMA(()),
        ],
        name="forces",
    )(own, even, odd)


def solution(mesh):
    placed = (
        P(None, "gx", "gy", "gz", None),
        P("gx", "gy", "gz", None),
        P("gx", "gy", "gz", None),
        P("gx", "gy", "gz"),
        P(),
        P(),
        P(None, "gx", "gy", "gz", None),
    )
    return jax.shard_map(
        per_device,
        mesh=mesh,
        in_specs=placed,
        out_specs=P(None, "gx", "gy", "gz", None),
        check_vma=False,
    )
```

time: 171 us -> 68 us (0.40)
  the two profiles are of different devices: /device:TPU:1 before, /device:TPU:31 now
where the time goes in v1:
time: 68 us; the launch traced here: 68.6 us
  blocking collectives  36.8 us (54%)
  Pallas kernels  31.8 us (47%)
    pallas_call x1, Pallas kernels, per_device(): pl.pallas_call(force_kernel, out_shape=jax.ShapeDtypeStruct((3, 2, 2, 2,...  28.5 us
    all_to_all x1, blocking collectives, per_device(): lax.all_to_all(send, AXES, 0, 0, axis_index_groups=swap_groups(sizes, 1),...  27.6 us
    all_to_all x1, blocking collectives, per_device(): lax.all_to_all(send, AXES, 0, 0, axis_index_groups=swap_groups(sizes, 0),...  9.18 us
    pallas_call x1, Pallas kernels, per_device(): pl.pallas_call(atoms_kernel, out_shape=(jax.ShapeDtypeStruct((8, 8, 128),...  1.66 us
    pallas_call x1, Pallas kernels, per_device(): pl.pallas_call(relay_kernel, out_shape=jax.ShapeDtypeStruct((8, 9, 8, 128...  1.66 us

profile of v1, /device:TPU:31, one launch (start us, length us, event | category | flops | bytes accessed | tf_op | source)
XLA Modules:
  0.0 68.6 jit_solution(15812974773779740803)
XLA Ops:
  0.0 1.7 %atoms.1 = (f32[8,8,128]{2,1,0:T(8,128)}, f32[8,4,8,128]{3,2,1,0:T(8,128)}) custom-call(f32[3,2,2,2,128]{4,3,2,1,0:T(2,128)} %pos_ref.1, f32[2,2,2,128]{3,2,1,0:T(2,128)} %charge_ref.1, s32[2,2,2,128]{3,2,1,0:T(2,128)} %type_ref.1, s32[2,2,2]{2,1,0:T(2,128)} %count_ref.1, f32[1,128]{1,0:T(1,128)} %bitcast.2, f32[1,128]{1,0:T(1,128)} %bitcast.3, ...), custom_call_target="tpu_custom_call" | custom-call | tf_op jit(solution)/shard_map/atoms/pallas_call | solution.py:238
  1.7 9.2 %all_to_all.10.got_ref.even_ref = f32[8,4,8,128]{3,2,1,0:T(8,128)} all-to-all(f32[8,4,8,128]{3,2,1,0:T(8,128)} %get-tuple-element.8), channel_id=1, replica_groups={{0,1,4,5,64,65,68,69},{2,3,6,7,66,67,70,71},{8,9,12,13,72,73,76,77},{10..., dimensions={0} | all-to-all | bytes 262144 | tf_op jit(solution)/shard_map/all_to_all | solution.py:246
  10.8 1.7 %relay.1 = f32[8,9,8,128]{3,2,1,0:T(8,128)} custom-call(f32[8,8,128]{2,1,0:T(8,128)} %get-tuple-element.7.own_ref, f32[8,4,8,128]{3,2,1,0:T(8,128)} %all_to_all.10.got_ref.even_ref), custom_call_target="tpu_custom_call" | custom-call | tf_op jit(solution)/shard_map/relay/pallas_call | solution.py:247
  12.5 27.6 %all_to_all.11.odd_ref = f32[8,9,8,128]{3,2,1,0:T(8,128)} all-to-all(f32[8,9,8,128]{3,2,1,0:T(8,128)} %relay.1), channel_id=1, replica_groups={{69,70,73,74,133,134,137,138},{71,68,75,72,135,132,139,136},{77,78,81,8..., dimensions={0} | all-to-all | bytes 589824 | tf_op jit(solution)/shard_map/all_to_all | solution.py:254
  40.1 28.5 %forces.1 = f32[3,2,2,2,128]{4,3,2,1,0:T(2,128)} custom-call(f32[8,8,128]{2,1,0:T(8,128)} %get-tuple-element.7.own_ref, f32[8,4,8,128]{3,2,1,0:T(8,128)} %all_to_all.10.got_ref.even_ref, f32[8,9,8,128]{3,2,1,0:T(8,128)} %all_to_all.11.odd_ref), custom_call_target="tpu_custom_call" | custom-call | tf_op jit(solution)/shard_map/forces/pallas_call | solution.py:255

commit v2 on v1

--- a/solution.py
+++ b/solution.py
@@ -16,13 +16,24 @@
 DEPTH_UNIT = math.sqrt(24.0)
 FORCE_UNIT = 2.0 / WIDTH * math.sqrt(WIDTH)
 COUNT_LANE = 27
+DONE_LANE = 28
 META_ROW = 6
 RELATIONS = [(r // 4, r // 2 % 2, r % 2) for r in range(1, 8)]
-MAX_CHUNKS = 30
+MAX_CHUNKS = 32
 
 
 def parities():
     return [lax.rem(lax.axis_index(name), 2) for name in AXES]
+
+
+def early_stages():
+    x, y, z = [lax.axis_index(name) for name in AXES]
+    last = lax.axis_size("gy") - 1
+    corner = jnp.maximum(x, jnp.maximum(y, z)) < 2
+    beside = jnp.logical_and(x < 3, jnp.logical_or(y < 3, y == last))
+    first = jnp.logical_and(corner, x + y + z > 0)
+    second = jnp.logical_and(jnp.logical_or(x == 0, beside), jnp.logical_not(corner))
+    return first, second
 
 
 def free_cells(relation, fixed, choices):
@@ -30,7 +41,7 @@
     return [(x, y, z) for x in spans[0] for y in spans[1] for z in spans[2]]
 
 
-def atoms_kernel(pos_ref, charge_ref, type_ref, count_ref, sigma_ref, eps_ref, pair_ref, own_ref, send_ref, rows_ref, kinds_ref, codes_ref):
+def atoms_kernel(pos_ref, charge_ref, type_ref, count_ref, sigma_ref, eps_ref, pair_ref, own_ref, send_ref, part_ref, rows_ref, kinds_ref, codes_ref, *work):
     for i in range(2):
         for j in range(2):
             at = pl.ds(4 * i + 2 * j, 2)
@@ -82,9 +93,16 @@
         slot = sum(lax.bitwise_xor(odd[a], rel[a]) * (4, 2, 1)[a] for a in range(3))
         for n, (x, y, z) in enumerate(free_cells(rel, toward, 2)):
             send_ref[slot, n] = own_ref[4 * x + 2 * y + z]
-
-
-def relay_kernel(own_ref, got_ref, send_ref):
+    part_ref[...] = jnp.zeros(part_ref.shape, jnp.float32)
+
+    @pl.when(early_stages()[0])
+    def _():
+        work[1][...] = jnp.zeros(work[1].shape, jnp.int32)
+        place(work[0], work[1], odd, own_ref, None, None)
+        cell_forces(part_ref, None, *work)
+
+
+def relay_kernel(own_ref, got_ref, before_ref, send_ref, part_ref, *work):
     odd = parities()
     for rel in RELATIONS:
         slot = sum(lax.bitwise_xor(1 - odd[a], rel[a]) * (4, 2, 1)[a] for a in range(3))
@@ -99,26 +117,36 @@
                 if not far[a]:
                     m = m * 2 + at[a]
             send_ref[slot, n] = got_ref[source, m]
-
-
-def place(ext_ref, meta_ref, own_ref, even_ref, odd_ref):
-    odd = parities()
+    part_ref[...] = before_ref[...]
+
+    @pl.when(early_stages()[1])
+    def _():
+        work[1][...] = jnp.zeros(work[1].shape, jnp.int32)
+        place(work[0], work[1], odd, own_ref, got_ref, None)
+        cell_forces(part_ref, None, *work)
+
+
+def place(ext_ref, meta_ref, odd, own_ref, even_ref, odd_ref, own_done=0, even_done=0):
     spot = [[1, 2, 3 - 3 * odd[a], 3 * odd[a]] for a in range(3)]
-
-    def put(at, tile):
+    lane = lax.broadcasted_iota(jnp.int32, (1, 128), 1)
+
+    def put(at, tile, done):
         where = spot[0][at[0]] * 16 + spot[1][at[1]] * 4 + spot[2][at[2]]
         ext_ref[where] = tile
-        meta_ref[pl.ds(where, 1), :] = tile[META_ROW:META_ROW + 1, :].astype(jnp.int32)
+        meta = tile[META_ROW:META_ROW + 1, :].astype(jnp.int32)
+        meta_ref[pl.ds(where, 1), :] = jnp.where(lane == DONE_LANE, done, meta)
 
     for c in range(8):
-        put((c // 4, c // 2 % 2, c % 2), own_ref[c])
+        put((c // 4, c // 2 % 2, c % 2), own_ref[c], own_done)
     for rel in RELATIONS:
-        slot = sum(lax.bitwise_xor(odd[a], rel[a]) * (4, 2, 1)[a] for a in range(3))
-        for n, at in enumerate(free_cells(rel, (2, 2, 2), 2)):
-            put(at, even_ref[slot, n])
-        slot = sum(lax.bitwise_xor(1 - odd[a], rel[a]) * (4, 2, 1)[a] for a in range(3))
-        for n, at in enumerate(free_cells(rel, (3, 3, 3), 3)):
-            put(at, odd_ref[slot, n])
+        if even_ref is not None:
+            slot = sum(lax.bitwise_xor(odd[a], rel[a]) * (4, 2, 1)[a] for a in range(3))
+            for n, at in enumerate(free_cells(rel, (2, 2, 2), 2)):
+                put(at, even_ref[slot, n], even_done)
+        if odd_ref is not None:
+            slot = sum(lax.bitwise_xor(1 - odd[a], rel[a]) * (4, 2, 1)[a] for a in range(3))
+            for n, at in enumerate(free_cells(rel, (3, 3, 3), 3)):
+                put(at, odd_ref[slot, n], 0)
 
 
 def pair_terms(home, other):
@@ -143,8 +171,18 @@
     return scale * dx, scale * dy, scale * dz
 
 
-def force_kernel(own_ref, even_ref, odd_ref, out_ref, ext_ref, meta_ref, info_ref, list_ref, cols_ref, sums_ref, rows_ref, sem):
-    place(ext_ref, meta_ref, own_ref, even_ref, odd_ref)
+WORK = [
+    pltpu.VMEM((64, 8, 128), jnp.float32),
+    pltpu.VMEM((64, 128), jnp.int32),
+    pltpu.SMEM((64, 128), jnp.int32),
+    pltpu.VMEM((MAX_CHUNKS, 8, 128), jnp.float32),
+    pltpu.VMEM((6, 128, 128), jnp.float32),
+    pltpu.VMEM((8, 3, 128, 128), jnp.float32),
+    pltpu.SemaphoreType.DMA(()),
+]
+
+
+def cell_forces(rows_ref, before_ref, ext_ref, meta_ref, info_ref, list_ref, home_ref, sums_ref, sem):
     copy = pltpu.make_async_copy(meta_ref, info_ref, sem)
     copy.start()
     copy.wait()
@@ -167,8 +205,8 @@
         for code in range(27):
             move = (code // 9 - 1, code // 3 % 3 - 1, code % 3 - 1)
             there = here + move[0] * 16 + move[1] * 4 + move[2]
-            listed = info_ref[here, code] + info_ref[there, 26 - code]
-            size = jnp.where(listed > 0, info_ref[there, COUNT_LANE], 0)
+            listed = info_ref[here, code] + info_ref[there, 26 - code] > 2 * info_ref[there, DONE_LANE]
+            size = jnp.where(listed, info_ref[there, COUNT_LANE], 0)
             chunk = lax.shift_right_logical(end, 7)
             first = lax.bitwise_and(end, 127)
             tile = pltpu.roll(ext_ref[there] + shift(move), first, axis=1)
@@ -179,42 +217,57 @@
         chunk = lax.shift_right_logical(end, 7)
         list_ref[chunk] = jnp.where(lane < lax.bitwise_and(end, 127), current, filler)
         list_ref[chunk + 1] = filler
-        rounds = lax.shift_right_logical(end + 255, 8)
-        cols_ref[...] = jnp.transpose(ext_ref[here])
-        sums_ref[...] = jnp.zeros(sums_ref.shape, jnp.float32)
+        pairs = lax.shift_right_logical(end + 255, 8)
+        cols = jnp.transpose(ext_ref[here])
+        for r in range(6):
+            home_ref[r] = jnp.broadcast_to(cols[:, r:r + 1], (128, 128))
+        sums_ref[c] = jnp.zeros(sums_ref.shape[1:], jnp.float32)
 
         def group_step(g, carry):
             first = pl.multiple_of(g * 16, 16)
             homes = []
             for h in range(2):
-                cols = cols_ref[pl.ds(first + 8 * h, 8), :]
-                homes.append([jnp.broadcast_to(cols[:, r:r + 1], (8, 128)) for r in range(6)])
-
-            def chunk_step(k, sums):
+                homes.append([home_ref[r, pl.ds(first + 8 * h, 8), :] for r in range(6)])
+
+            def chunk_step(start, width, sums):
                 sums = list(sums)
-                for u in range(2):
-                    other = [jnp.broadcast_to(list_ref[2 * k + u, r:r + 1, :], (8, 128)) for r in range(6)]
+                for u in range(width):
+                    other = [jnp.broadcast_to(list_ref[start + u, r:r + 1, :], (8, 128)) for r in range(6)]
                     for h in range(2):
                         terms = pair_terms(homes[h], other)
                         for a in range(3):
                             sums[3 * h + a] = sums[3 * h + a] + terms[a]
                 return tuple(sums)
 
-            sums = lax.fori_loop(0, rounds, chunk_step, (jnp.zeros((8, 128), jnp.float32),) * 6)
+            fours = lax.shift_right_logical(pairs, 1)
+            sums = (jnp.zeros((8, 128), jnp.float32),) * 6
+            sums = lax.fori_loop(0, fours, lambda k, x: chunk_step(4 * k, 4, x), sums)
+            sums = lax.fori_loop(2 * fours, pairs, lambda k, x: chunk_step(2 * k, 2, x), sums)
             for h in range(2):
-                total = [jnp.sum(sums[3 * h + a], axis=1, keepdims=True) for a in range(3)]
-                line = jnp.where(lane == 0, total[0], jnp.where(lane == 1, total[1], total[2]))
-                sums_ref[pl.ds(first + 8 * h, 8), :] = line[:, 0:8]
+                for a in range(3):
+                    sums_ref[c, a, pl.ds(first + 8 * h, 8), :] = sums[3 * h + a]
             return carry
 
         lax.fori_loop(0, lax.shift_right_logical(atoms + 15, 4), group_step, 0)
-        rows_ref[c] = jnp.transpose(sums_ref[...]) * FORCE_UNIT
         return carry
 
     lax.fori_loop(0, 8, cell_step, 0)
+    comp = lax.broadcasted_iota(jnp.int32, (128, 8), 1)
+    for c in range(8):
+        total = [jnp.sum(sums_ref[c, a], axis=1, keepdims=True) for a in range(3)]
+        line = jnp.where(comp == 0, total[0], jnp.where(comp == 1, total[1], total[2]))
+        rows = jnp.transpose(line)
+        rows_ref[c] = rows if before_ref is None else rows + before_ref[c]
+
+
+def force_kernel(own_ref, even_ref, odd_ref, before_ref, out_ref, rows_ref, *work):
+    first, second = early_stages()
+    own_done = jnp.where(jnp.logical_or(first, second), 1, 0)
+    place(work[0], work[1], parities(), own_ref, even_ref, odd_ref, own_done, jnp.where(second, 1, 0))
+    cell_forces(rows_ref, before_ref, *work)
     for c in range(8):
         for a in range(3):
-            out_ref[a, c // 4, c // 2 % 2, c % 2:c % 2 + 1, :] = rows_ref[c, a:a + 1, :]
+            out_ref[a, c // 4, c // 2 % 2, c % 2:c % 2 + 1, :] = rows_ref[c, a:a + 1, :] * FORCE_UNIT
 
 
 def swap_groups(sizes, start):
@@ -235,40 +288,33 @@
     sizes = [lax.axis_size(name) for name in AXES]
     vmem = pl.BlockSpec(memory_space=pltpu.VMEM)
     smem = pl.BlockSpec(memory_space=pltpu.SMEM)
-    own, send = pl.pallas_call(
+    part_shape = jax.ShapeDtypeStruct((8, 8, 128), f32)
+    own, send, part = pl.pallas_call(
         atoms_kernel,
-        out_shape=(jax.ShapeDtypeStruct((8, 8, 128), f32), jax.ShapeDtypeStruct((8, 4, 8, 128), f32)),
+        out_shape=(part_shape, jax.ShapeDtypeStruct((8, 4, 8, 128), f32), part_shape),
         in_specs=[vmem, vmem, vmem, smem, vmem, vmem, vmem],
-        out_specs=(vmem, vmem),
-        scratch_shapes=[pltpu.VMEM((4, 8, 128), f32), pltpu.VMEM((8, 128), jnp.int32), pltpu.VMEM((8, 256), jnp.int32)],
+        out_specs=(vmem, vmem, vmem),
+        scratch_shapes=[pltpu.VMEM((4, 8, 128), f32), pltpu.VMEM((8, 128), jnp.int32), pltpu.VMEM((8, 256), jnp.int32)] + WORK,
         name="atoms",
     )(positions, charges, atom_types, atom_counts, type_sigma.reshape(1, -1), type_epsilon.reshape(1, -1), pair_list)
     even = lax.all_to_all(send, AXES, 0, 0, axis_index_groups=swap_groups(sizes, 0), tiled=True)
-    send = pl.pallas_call(
+    send, part = pl.pallas_call(
         relay_kernel,
-        out_shape=jax.ShapeDtypeStruct((8, 9, 8, 128), f32),
-        in_specs=[vmem, vmem],
-        out_specs=vmem,
+        out_shape=(jax.ShapeDtypeStruct((8, 9, 8, 128), f32), part_shape),
+        in_specs=[vmem, vmem, vmem],
+        out_specs=(vmem, vmem),
+        scratch_shapes=WORK,
         name="relay",
-    )(own, even)
+    )(own, even, part)
     odd = lax.all_to_all(send, AXES, 0, 0, axis_index_groups=swap_groups(sizes, 1), tiled=True)
     return pl.pallas_call(
         force_kernel,
         out_shape=jax.ShapeDtypeStruct((3, 2, 2, 2, 128), f32),
-        in_specs=[vmem, vmem, vmem],
+        in_specs=[vmem] * 4,
         out_specs=vmem,
-        scratch_shapes=[
-            pltpu.VMEM((64, 8, 128), f32),
-            pltpu.VMEM((64, 128), jnp.int32),
-            pltpu.SMEM((64, 128), jnp.int32),
-            pltpu.VMEM((MAX_CHUNKS, 8, 128), f32),
-            pltpu.VMEM((128, 8), f32),
-            pltpu.VMEM((128, 8), f32),
-            pltpu.VMEM((8, 8, 128), f32),
-            pltpu.SemaphoreType.DMA(()),
-        ],
+        scratch_shapes=[pltpu.VMEM((8, 8, 128), f32)] + WORK,
         name="forces",
-    )(own, even, odd)
+    )(own, even, odd, part)
 
 
 def solution(mesh):

time: 68 us -> 55.6 us (0.82)
  the two profiles are of different devices: /device:TPU:31 before, /device:TPU:2 now
where the time goes in v2:
time: 55.6 us; the launch traced here: 55.2 us
  Pallas kernels  29.8 us (54%)
  blocking collectives  25.4 us (46%)
    pallas_call x1, Pallas kernels, per_device(): pl.pallas_call(force_kernel, out_shape=jax.ShapeDtypeStruct((3, 2, 2, 2,...  15.7 us
    all_to_all x1, blocking collectives, per_device(): lax.all_to_all(send, AXES, 0, 0, axis_index_groups=swap_groups(sizes, 1),...  14.9 us
    pallas_call x1, Pallas kernels, per_device(): pl.pallas_call(atoms_kernel, out_shape=(part_shape, jax.ShapeDtypeStruct(...  12.4 us
    all_to_all x1, blocking collectives, per_device(): lax.all_to_all(send, AXES, 0, 0, axis_index_groups=swap_groups(sizes, 0),...  10.5 us
    pallas_call x1, Pallas kernels, per_device(): pl.pallas_call(relay_kernel, out_shape=(jax.ShapeDtypeStruct((8, 9, 8, 12...  1.66 us

profile of v2, /device:TPU:2, one launch (start us, length us, event | category | flops | bytes accessed | tf_op | source)
XLA Modules:
  0.0 55.2 jit_solution(10630268965818503576)
XLA Ops:
  0.0 12.4 %atoms.1 = (f32[8,8,128]{2,1,0:T(8,128)}, f32[8,4,8,128]{3,2,1,0:T(8,128)}, f32[8,8,128]{2,1,0:T(8,128)}) custom-call(f32[3,2,2,2,128]{4,3,2,1,0:T(2,128)} %pos_ref.1, f32[2,2,2,128]{3,2,1,0:T(2,128)} %charge_ref.1, s32[2,2,2,128]{3,2,1,0:T(2,128)} %type_ref.1, s32[2,2,2]{2,1,0:T(2,128)} %count_ref.1, f32[1,128]{1,0:T(1,128)} %bitcast.2, f32[1,128]{1,0:T(1,128)} %bitcast.3, ...), custom_call_target="tpu_custom_call" | custom-call | tf_op jit(solution)/shard_map/atoms/pallas_call | solution.py:292
  12.4 10.5 %all_to_all.10.got_ref.even_ref = f32[8,4,8,128]{3,2,1,0:T(8,128)} all-to-all(f32[8,4,8,128]{3,2,1,0:T(8,128)} %get-tuple-element.11), channel_id=1, replica_groups={{0,1,4,5,64,65,68,69},{2,3,6,7,66,67,70,71},{8,9,12,13,72,73,76,77},{10..., dimensions={0} | all-to-all | bytes 262144 | tf_op jit(solution)/shard_map/all_to_all | solution.py:300
  22.9 1.7 %relay.1 = (f32[8,9,8,128]{3,2,1,0:T(8,128)}, f32[8,8,128]{2,1,0:T(8,128)}) custom-call(f32[8,8,128]{2,1,0:T(8,128)} %get-tuple-element.10.own_ref, f32[8,4,8,128]{3,2,1,0:T(8,128)} %all_to_all.10.got_ref.even_ref, f32[8,8,128]{2,1,0:T(8,128)} %get-tuple-element.12.before_ref), custom_call_target="tpu_custom_call" | custom-call | tf_op jit(solution)/shard_map/relay/pallas_call | solution.py:301
  24.6 14.9 %all_to_all.11.odd_ref = f32[8,9,8,128]{3,2,1,0:T(8,128)} all-to-all(f32[8,9,8,128]{3,2,1,0:T(8,128)} %get-tuple-element.13), channel_id=1, replica_groups={{69,70,73,74,133,134,137,138},{71,68,75,72,135,132,139,136},{77,78,81,8..., dimensions={0} | all-to-all | bytes 589824 | tf_op jit(solution)/shard_map/all_to_all | solution.py:309
  39.5 15.7 %forces.1 = f32[3,2,2,2,128]{4,3,2,1,0:T(2,128)} custom-call(f32[8,8,128]{2,1,0:T(8,128)} %get-tuple-element.10.own_ref, f32[8,4,8,128]{3,2,1,0:T(8,128)} %all_to_all.10.got_ref.even_ref, f32[8,9,8,128]{3,2,1,0:T(8,128)} %all_to_all.11.odd_ref, f32[8,8,128]{2,1,0:T(8,128)} %get-tuple-element.14.before_ref), custom_call_target="tpu_custom_call" | custom-call | tf_op jit(solution)/shard_map/forces/pallas_call | solution.py:310

commit v3 on v2

--- a/solution.py
+++ b/solution.py
@@ -176,7 +176,7 @@
     pltpu.VMEM((64, 128), jnp.int32),
     pltpu.SMEM((64, 128), jnp.int32),
     pltpu.VMEM((MAX_CHUNKS, 8, 128), jnp.float32),
-    pltpu.VMEM((6, 128, 128), jnp.float32),
+    pltpu.VMEM((8, 6, 128, 128), jnp.float32),
     pltpu.VMEM((8, 3, 128, 128), jnp.float32),
     pltpu.SemaphoreType.DMA(()),
 ]
@@ -185,6 +185,10 @@
 def cell_forces(rows_ref, before_ref, ext_ref, meta_ref, info_ref, list_ref, home_ref, sums_ref, sem):
     copy = pltpu.make_async_copy(meta_ref, info_ref, sem)
     copy.start()
+    for c in range(8):
+        cols = jnp.transpose(ext_ref[(1 + c // 4) * 16 + (1 + c // 2 % 2) * 4 + 1 + c % 2])
+        for r in range(6):
+            home_ref[c, r] = jnp.broadcast_to(cols[:, r:r + 1], (128, 128))
     copy.wait()
     lane = lax.broadcasted_iota(jnp.int32, (8, 128), 1)
     row = lax.broadcasted_iota(jnp.int32, (8, 128), 0)
@@ -218,16 +222,12 @@
         list_ref[chunk] = jnp.where(lane < lax.bitwise_and(end, 127), current, filler)
         list_ref[chunk + 1] = filler
         pairs = lax.shift_right_logical(end + 255, 8)
-        cols = jnp.transpose(ext_ref[here])
-        for r in range(6):
-            home_ref[r] = jnp.broadcast_to(cols[:, r:r + 1], (128, 128))
-        sums_ref[c] = jnp.zeros(sums_ref.shape[1:], jnp.float32)
 
         def group_step(g, carry):
             first = pl.multiple_of(g * 16, 16)
             homes = []
             for h in range(2):
-                homes.append([home_ref[r, pl.ds(first + 8 * h, 8), :] for r in range(6)])
+                homes.append([home_ref[c, r, pl.ds(first + 8 * h, 8), :] for r in range(6)])
 
             def chunk_step(start, width, sums):
                 sums = list(sums)
@@ -256,7 +256,8 @@
     for c in range(8):
         total = [jnp.sum(sums_ref[c, a], axis=1, keepdims=True) for a in range(3)]
         line = jnp.where(comp == 0, total[0], jnp.where(comp == 1, total[1], total[2]))
-        rows = jnp.transpose(line)
+        atoms = info_ref[(1 + c // 4) * 16 + (1 + c // 2 % 2) * 4 + 1 + c % 2, COUNT_LANE]
+        rows = jnp.where(lane < atoms, jnp.transpose(line), 0.0)
         rows_ref[c] = rows if before_ref is None else rows + before_ref[c]
 
 
@@ -288,10 +289,11 @@
     sizes = [lax.axis_size(name) for name in AXES]
     vmem = pl.BlockSpec(memory_space=pltpu.VMEM)
     smem = pl.BlockSpec(memory_space=pltpu.SMEM)
-    part_shape = jax.ShapeDtypeStruct((8, 8, 128), f32)
+    part_shape = pltpu.VMEM((8, 8, 128), f32)
+    keep = lambda x: pltpu.with_memory_space_constraint(x, pltpu.VMEM)
     own, send, part = pl.pallas_call(
         atoms_kernel,
-        out_shape=(part_shape, jax.ShapeDtypeStruct((8, 4, 8, 128), f32), part_shape),
+        out_shape=(part_shape, pltpu.VMEM((8, 4, 8, 128), f32), part_shape),
         in_specs=[vmem, vmem, vmem, smem, vmem, vmem, vmem],
         out_specs=(vmem, vmem, vmem),
         scratch_shapes=[pltpu.VMEM((4, 8, 128), f32), pltpu.VMEM((8, 128), jnp.int32), pltpu.VMEM((8, 256), jnp.int32)] + WORK,
@@ -300,12 +302,12 @@
     even = lax.all_to_all(send, AXES, 0, 0, axis_index_groups=swap_groups(sizes, 0), tiled=True)
     send, part = pl.pallas_call(
         relay_kernel,
-        out_shape=(jax.ShapeDtypeStruct((8, 9, 8, 128), f32), part_shape),
+        out_shape=(pltpu.VMEM((8, 9, 8, 128), f32), part_shape),
         in_specs=[vmem, vmem, vmem],
         out_specs=(vmem, vmem),
         scratch_shapes=WORK,
         name="relay",
-    )(own, even, part)
+    )(keep(own), keep(even), keep(part))
     odd = lax.all_to_all(send, AXES, 0, 0, axis_index_groups=swap_groups(sizes, 1), tiled=True)
     return pl.pallas_call(
         force_kernel,
@@ -314,7 +316,7 @@
         out_specs=vmem,
         scratch_shapes=[pltpu.VMEM((8, 8, 128), f32)] + WORK,
         name="forces",
-    )(own, even, odd, part)
+    )(keep(own), keep(even), keep(odd), keep(part))
 
 
 def solution(mesh):

time: 55.6 us -> 48.2 us (0.87)
  the two profiles are of different devices: /device:TPU:2 before, /device:TPU:1 now
where the time goes in v3:
time: 48.2 us; the launch traced here: 48.1 us
  blocking collectives  27.9 us (58%)
  Pallas kernels  20.2 us (42%)
    all_to_all x1, blocking collectives, per_device(): lax.all_to_all(send, AXES, 0, 0, axis_index_groups=swap_groups(sizes, 1),...  14.1 us
    all_to_all x1, blocking collectives, per_device(): lax.all_to_all(send, AXES, 0, 0, axis_index_groups=swap_groups(sizes, 0),...  13.8 us
    pallas_call x1, Pallas kernels, per_device(): pl.pallas_call(force_kernel, out_shape=jax.ShapeDtypeStruct((3, 2, 2, 2,...  11.8 us
    pallas_call x1, Pallas kernels, per_device(): pl.pallas_call(atoms_kernel, out_shape=(part_shape, pltpu.VMEM((8, 4, 8,...  8.33 us

profile of v3, /device:TPU:1, one launch (start us, length us, event | category | flops | bytes accessed | tf_op | source)
XLA Modules:
  0.0 48.1 jit_solution(1496228290961451051)
XLA Ops:
  0.0 8.3 %atoms.1 = (f32[8,8,128]{2,1,0:T(8,128)S(1)}, f32[8,4,8,128]{3,2,1,0:T(8,128)S(1)}, f32[8,8,128]{2,1,0:T(8,128)S(1)}) custom-call(f32[3,2,2,2,128]{4,3,2,1,0:T(2,128)} %pos_ref.1, f32[2,2,2,128]{3,2,1,0:T(2,128)} %charge_ref.1, s32[2,2,2,128]{3,2,1,0:T(2,128)} %type_ref.1, s32[2,2,2]{2,1,0:T(2,128)} %count_ref.1, f32[1,128]{1,0:T(1,128)} %bitcast.2, ...), custom_call_target="tpu_custom_call" | custom-call | tf_op jit(solution)/shard_map/atoms/pallas_call | solution.py:294
  8.3 13.8 %all_to_all.10.got_ref.even_ref = f32[8,4,8,128]{3,2,1,0:T(8,128)S(1)} all-to-all(f32[8,4,8,128]{3,2,1,0:T(8,128)S(1)} %get-tuple-element.11), channel_id=1, replica_groups={{0,1,4,5,64,65,68,69},{2,3,6,7,66,67,70,71},{8,9,12,13,72,73,76,77},{10..., dimensions={0} | all-to-all | bytes 262144 | tf_op jit(solution)/shard_map/all_to_all | solution.py:302
  22.2 14.1 %all_to_all.11.odd_ref = f32[8,9,8,128]{3,2,1,0:T(8,128)S(1)} all-to-all(f32[8,9,8,128]{3,2,1,0:T(8,128)S(1)} %get-tuple-element.13), channel_id=1, replica_groups={{69,70,73,74,133,134,137,138},{71,68,75,72,135,132,139,136},{77,78,81,8..., dimensions={0} | all-to-all | bytes 589824 | tf_op jit(solution)/shard_map/all_to_all | solution.py:311
  36.3 11.8 %forces.1 = f32[3,2,2,2,128]{4,3,2,1,0:T(2,128)} custom-call(f32[8,8,128]{2,1,0:T(8,128)S(1)} %get-tuple-element.10.own_ref, f32[8,4,8,128]{3,2,1,0:T(8,128)S(1)} %all_to_all.10.got_ref.even_ref, f32[8,9,8,128]{3,2,1,0:T(8,128)S(1)} %all_to_all.11.odd_ref, f32[8,8,128]{2,1,0:T(8,128)S(1)} %get-tuple-element.14.before_ref), custom_call_target="tpu_custom_call" | custom-call | tf_op jit(solution)/shard_map/forces/pallas_call | solution.py:312
  (1 shorter events, 0.0 us)

commit v4 on v3

--- a/solution.py
+++ b/solution.py
@@ -8,6 +8,7 @@
 from jax.sharding import PartitionSpec as P
 
 AXES = ("gx", "gy", "gz")
+FIRST_PAIRS = (1, 0, 0)
 CUT = 144.0
 WIDTH = 44.0
 UNIT = 1.0 / math.sqrt(WIDTH)
@@ -16,24 +17,19 @@
 DEPTH_UNIT = math.sqrt(24.0)
 FORCE_UNIT = 2.0 / WIDTH * math.sqrt(WIDTH)
 COUNT_LANE = 27
-DONE_LANE = 28
+LEFT_LANE = 28
 META_ROW = 6
 RELATIONS = [(r // 4, r // 2 % 2, r % 2) for r in range(1, 8)]
 MAX_CHUNKS = 32
 
 
 def parities():
-    return [lax.rem(lax.axis_index(name), 2) for name in AXES]
+    return [lax.rem(lax.axis_index(name) + start, 2) for name, start in zip(AXES, FIRST_PAIRS)]
 
 
 def early_stages():
     x, y, z = [lax.axis_index(name) for name in AXES]
-    last = lax.axis_size("gy") - 1
-    corner = jnp.maximum(x, jnp.maximum(y, z)) < 2
-    beside = jnp.logical_and(x < 3, jnp.logical_or(y < 3, y == last))
-    first = jnp.logical_and(corner, x + y + z > 0)
-    second = jnp.logical_and(jnp.logical_or(x == 0, beside), jnp.logical_not(corner))
-    return first, second
+    return jnp.logical_and(x == 0, y + z > 0), x == 1
 
 
 def free_cells(relation, fixed, choices):
@@ -77,7 +73,8 @@
         (((1,), (1,)), ((), ())),
         preferred_element_type=jnp.float32,
     )
-    meta = jnp.where(lane == COUNT_LANE, count.astype(jnp.float32), listed)
+    atoms = count.astype(jnp.float32)
+    meta = jnp.where(jnp.logical_or(lane == COUNT_LANE, lane == LEFT_LANE), atoms, listed * atoms)
 
     values = [rows_ref[0] * UNIT, rows_ref[1] * UNIT, rows_ref[2] * UNIT]
     values.append(jnp.where(live, rows_ref[3] * CHARGE_UNIT, 0.0))
@@ -99,7 +96,7 @@
     def _():
         work[1][...] = jnp.zeros(work[1].shape, jnp.int32)
         place(work[0], work[1], odd, own_ref, None, None)
-        cell_forces(part_ref, None, *work)
+        cell_forces(part_ref, None, None, *work)
 
 
 def relay_kernel(own_ref, got_ref, before_ref, send_ref, part_ref, *work):
@@ -123,10 +120,10 @@
     def _():
         work[1][...] = jnp.zeros(work[1].shape, jnp.int32)
         place(work[0], work[1], odd, own_ref, got_ref, None)
-        cell_forces(part_ref, None, *work)
-
-
-def place(ext_ref, meta_ref, odd, own_ref, even_ref, odd_ref, own_done=0, even_done=0):
+        cell_forces(part_ref, None, None, *work)
+
+
+def place(ext_ref, meta_ref, odd, own_ref, even_ref, odd_ref, even_done=0):
     spot = [[1, 2, 3 - 3 * odd[a], 3 * odd[a]] for a in range(3)]
     lane = lax.broadcasted_iota(jnp.int32, (1, 128), 1)
 
@@ -134,10 +131,10 @@
         where = spot[0][at[0]] * 16 + spot[1][at[1]] * 4 + spot[2][at[2]]
         ext_ref[where] = tile
         meta = tile[META_ROW:META_ROW + 1, :].astype(jnp.int32)
-        meta_ref[pl.ds(where, 1), :] = jnp.where(lane == DONE_LANE, done, meta)
-
-    for c in range(8):
-        put((c // 4, c // 2 % 2, c % 2), own_ref[c], own_done)
+        meta_ref[pl.ds(where, 1), :] = jnp.where(jnp.logical_and(lane != COUNT_LANE, done > 0), 0, meta)
+
+    for c in range(8):
+        put((c // 4, c // 2 % 2, c % 2), own_ref[c], 0)
     for rel in RELATIONS:
         if even_ref is not None:
             slot = sum(lax.bitwise_xor(odd[a], rel[a]) * (4, 2, 1)[a] for a in range(3))
@@ -175,20 +172,36 @@
     pltpu.VMEM((64, 8, 128), jnp.float32),
     pltpu.VMEM((64, 128), jnp.int32),
     pltpu.SMEM((64, 128), jnp.int32),
-    pltpu.VMEM((MAX_CHUNKS, 8, 128), jnp.float32),
+    pltpu.VMEM((8, MAX_CHUNKS, 8, 128), jnp.float32),
+    pltpu.SMEM((8,), jnp.int32),
     pltpu.VMEM((8, 6, 128, 128), jnp.float32),
     pltpu.VMEM((8, 3, 128, 128), jnp.float32),
     pltpu.SemaphoreType.DMA(()),
 ]
 
 
-def cell_forces(rows_ref, before_ref, ext_ref, meta_ref, info_ref, list_ref, home_ref, sums_ref, sem):
+def spatial(c):
+    return (1 + c // 4) * 16 + (1 + c // 2 % 2) * 4 + 1 + c % 2
+
+
+def cell_forces(rows_ref, before_ref, own_done, ext_ref, meta_ref, info_ref, list_ref, pairs_ref, home_ref, sums_ref, sem):
     copy = pltpu.make_async_copy(meta_ref, info_ref, sem)
     copy.start()
-    for c in range(8):
-        cols = jnp.transpose(ext_ref[(1 + c // 4) * 16 + (1 + c // 2 % 2) * 4 + 1 + c % 2])
+    part = lax.broadcasted_iota(jnp.int32, (32, 768), 0)
+    column = lax.broadcasted_iota(jnp.int32, (32, 768), 1)
+    pick = jnp.logical_and(lax.bitwise_and(part, 7) == lax.shift_right_logical(column, 7), part < 24)
+    pick = jnp.where(pick, 1.0, 0.0).astype(jnp.bfloat16)
+    for c in range(8):
+        rest = ext_ref[spatial(c)]
+        pieces = []
+        for _ in range(3):
+            pieces.append(rest.astype(jnp.bfloat16).astype(jnp.float32))
+            rest = rest - pieces[-1]
+        pieces.append(jnp.zeros((8, 128), jnp.float32))
+        cols = jnp.transpose(jnp.concatenate(pieces, 0)).astype(jnp.bfloat16)
+        wide = lax.dot_general(cols, pick, (((1,), (0,)), ((), ())), preferred_element_type=jnp.float32)
         for r in range(6):
-            home_ref[c, r] = jnp.broadcast_to(cols[:, r:r + 1], (128, 128))
+            home_ref[c, r] = wide[:, 128 * r:128 * (r + 1)]
     copy.wait()
     lane = lax.broadcasted_iota(jnp.int32, (8, 128), 1)
     row = lax.broadcasted_iota(jnp.int32, (8, 128), 0)
@@ -201,27 +214,33 @@
                 vector = jnp.where(row == a, move[a] * EDGE, vector)
         return vector
 
-    def cell_step(c, carry):
-        here = (1 + c // 4) * 16 + (1 + c // 2 % 2) * 4 + 1 + c % 2
-        atoms = info_ref[here, COUNT_LANE]
+    own_spots = [spatial(c) for c in range(8)]
+    for c in range(8):
+        here = spatial(c)
         end = jnp.int32(0)
         current = filler
         for code in range(27):
             move = (code // 9 - 1, code // 3 % 3 - 1, code % 3 - 1)
             there = here + move[0] * 16 + move[1] * 4 + move[2]
-            listed = info_ref[here, code] + info_ref[there, 26 - code] > 2 * info_ref[there, DONE_LANE]
-            size = jnp.where(listed, info_ref[there, COUNT_LANE], 0)
+            size = jnp.where(info_ref[here, code] > 0, info_ref[there, LEFT_LANE], info_ref[there, 26 - code])
+            if own_done is not None and there in own_spots:
+                size = jnp.where(own_done, 0, size)
             chunk = lax.shift_right_logical(end, 7)
             first = lax.bitwise_and(end, 127)
             tile = pltpu.roll(ext_ref[there] + shift(move), first, axis=1)
             merged = jnp.where(lane < first, current, tile)
-            list_ref[chunk] = merged
+            list_ref[c, chunk] = merged
             end = end + size
             current = jnp.where(lax.shift_right_logical(end, 7) > chunk, tile, merged)
         chunk = lax.shift_right_logical(end, 7)
-        list_ref[chunk] = jnp.where(lane < lax.bitwise_and(end, 127), current, filler)
-        list_ref[chunk + 1] = filler
-        pairs = lax.shift_right_logical(end + 255, 8)
+        list_ref[c, chunk] = jnp.where(lane < lax.bitwise_and(end, 127), current, filler)
+        list_ref[c, chunk + 1] = filler
+        pairs_ref[c] = lax.shift_right_logical(end + 255, 8)
+
+    def cell_step(c, carry):
+        here = (1 + c // 4) * 16 + (1 + c // 2 % 2) * 4 + 1 + c % 2
+        atoms = info_ref[here, COUNT_LANE]
+        pairs = pairs_ref[c]
 
         def group_step(g, carry):
             first = pl.multiple_of(g * 16, 16)
@@ -232,7 +251,7 @@
             def chunk_step(start, width, sums):
                 sums = list(sums)
                 for u in range(width):
-                    other = [jnp.broadcast_to(list_ref[start + u, r:r + 1, :], (8, 128)) for r in range(6)]
+                    other = [jnp.broadcast_to(list_ref[c, start + u, r:r + 1, :], (8, 128)) for r in range(6)]
                     for h in range(2):
                         terms = pair_terms(homes[h], other)
                         for a in range(3):
@@ -256,16 +275,15 @@
     for c in range(8):
         total = [jnp.sum(sums_ref[c, a], axis=1, keepdims=True) for a in range(3)]
         line = jnp.where(comp == 0, total[0], jnp.where(comp == 1, total[1], total[2]))
-        atoms = info_ref[(1 + c // 4) * 16 + (1 + c // 2 % 2) * 4 + 1 + c % 2, COUNT_LANE]
+        atoms = info_ref[spatial(c), COUNT_LANE]
         rows = jnp.where(lane < atoms, jnp.transpose(line), 0.0)
         rows_ref[c] = rows if before_ref is None else rows + before_ref[c]
 
 
 def force_kernel(own_ref, even_ref, odd_ref, before_ref, out_ref, rows_ref, *work):
     first, second = early_stages()
-    own_done = jnp.where(jnp.logical_or(first, second), 1, 0)
-    place(work[0], work[1], parities(), own_ref, even_ref, odd_ref, own_done, jnp.where(second, 1, 0))
-    cell_forces(rows_ref, before_ref, *work)
+    place(work[0], work[1], parities(), own_ref, even_ref, odd_ref, jnp.where(second, 1, 0))
+    cell_forces(rows_ref, before_ref, jnp.logical_or(first, second), *work)
     for c in range(8):
         for a in range(3):
             out_ref[a, c // 4, c // 2 % 2, c % 2:c % 2 + 1, :] = rows_ref[c, a:a + 1, :] * FORCE_UNIT
@@ -277,7 +295,7 @@
 
     bits = [(b // 4, b // 2 % 2, b % 2) for b in range(8)]
     return [
-        [index(x + start + bx, y + start + by, z + start + bz) for bx, by, bz in bits]
+        [index(x + start[0] + bx, y + start[1] + by, z + start[2] + bz) for bx, by, bz in bits]
         for x in range(0, sizes[0], 2)
         for y in range(0, sizes[1], 2)
         for z in range(0, sizes[2], 2)
@@ -299,7 +317,7 @@
         scratch_shapes=[pltpu.VMEM((4, 8, 128), f32), pltpu.VMEM((8, 128), jnp.int32), pltpu.VMEM((8, 256), jnp.int32)] + WORK,
         name="atoms",
     )(positions, charges, atom_types, atom_counts, type_sigma.reshape(1, -1), type_epsilon.reshape(1, -1), pair_list)
-    even = lax.all_to_all(send, AXES, 0, 0, axis_index_groups=swap_groups(sizes, 0), tiled=True)
+    even = lax.all_to_all(send, AXES, 0, 0, axis_index_groups=swap_groups(sizes, FIRST_PAIRS), tiled=True)
     send, part = pl.pallas_call(
         relay_kernel,
         out_shape=(pltpu.VMEM((8, 9, 8, 128), f32), part_shape),
@@ -308,7 +326,7 @@
         scratch_shapes=WORK,
         name="relay",
     )(keep(own), keep(even), keep(part))
-    odd = lax.all_to_all(send, AXES, 0, 0, axis_index_groups=swap_groups(sizes, 1), tiled=True)
+    odd = lax.all_to_all(send, AXES, 0, 0, axis_index_groups=swap_groups(sizes, [1 - start for start in FIRST_PAIRS]), tiled=True)
     return pl.pallas_call(
         force_kernel,
         out_shape=jax.ShapeDtypeStruct((3, 2, 2, 2, 128), f32),

time: 48.2 us -> 49.2 us (1.021)
  the two profiles are of different devices: /device:TPU:1 before, /device:TPU:27 now
where the time goes in v4:
time: 49.2 us; the launch traced here: 48.5 us
  blocking collectives  27.3 us (55%)
  Pallas kernels  21.2 us (43%)
    all_to_all x1, blocking collectives, per_device(): lax.all_to_all(send, AXES, 0, 0, axis_index_groups=swap_groups(sizes, FIR...  14 us
    all_to_all x1, blocking collectives, per_device(): lax.all_to_all(send, AXES, 0, 0, axis_index_groups=swap_groups(sizes, [1...  13.3 us
    pallas_call x1, Pallas kernels, per_device(): pl.pallas_call(force_kernel, out_shape=jax.ShapeDtypeStruct((3, 2, 2, 2,...  12.3 us
    pallas_call x1, Pallas kernels, per_device(): pl.pallas_call(atoms_kernel, out_shape=(part_shape, pltpu.VMEM((8, 4, 8,...  8.95 us

profile of v4, /device:TPU:27, one launch (start us, length us, event | category | flops | bytes accessed | tf_op | source)
XLA Modules:
  0.0 48.5 jit_solution(13249860705261014856)
XLA Ops:
  0.0 9.0 %atoms.1 = (f32[8,8,128]{2,1,0:T(8,128)S(1)}, f32[8,4,8,128]{3,2,1,0:T(8,128)S(1)}, f32[8,8,128]{2,1,0:T(8,128)S(1)}) custom-call(f32[3,2,2,2,128]{4,3,2,1,0:T(2,128)} %pos_ref.1, f32[2,2,2,128]{3,2,1,0:T(2,128)} %charge_ref.1, s32[2,2,2,128]{3,2,1,0:T(2,128)} %type_ref.1, s32[2,2,2]{2,1,0:T(2,128)} %count_ref.1, f32[1,128]{1,0:T(1,128)} %bitcast.2, ...), custom_call_target="tpu_custom_call" | custom-call | tf_op jit(solution)/shard_map/atoms/pallas_call | solution.py:312
  9.0 14.0 %all_to_all.10.got_ref.even_ref = f32[8,4,8,128]{3,2,1,0:T(8,128)S(1)} all-to-all(f32[8,4,8,128]{3,2,1,0:T(8,128)S(1)} %get-tuple-element.11), channel_id=1, replica_groups={{64,65,68,69,128,129,132,133},{66,67,70,71,130,131,134,135},{72,73,76,7..., dimensions={0} | all-to-all | bytes 262144 | tf_op jit(solution)/shard_map/all_to_all | solution.py:320
  23.0 13.3 %all_to_all.11.odd_ref = f32[8,9,8,128]{3,2,1,0:T(8,128)S(1)} all-to-all(f32[8,9,8,128]{3,2,1,0:T(8,128)S(1)} %get-tuple-element.13), channel_id=1, replica_groups={{5,6,9,10,69,70,73,74},{7,4,11,8,71,68,75,72},{13,14,17,18,77,78,81,82}..., dimensions={0} | all-to-all | bytes 589824 | tf_op jit(solution)/shard_map/all_to_all | solution.py:329
  36.3 12.3 %forces.1 = f32[3,2,2,2,128]{4,3,2,1,0:T(2,128)} custom-call(f32[8,8,128]{2,1,0:T(8,128)S(1)} %get-tuple-element.10.own_ref, f32[8,4,8,128]{3,2,1,0:T(8,128)S(1)} %all_to_all.10.got_ref.even_ref, f32[8,9,8,128]{3,2,1,0:T(8,128)S(1)} %all_to_all.11.odd_ref, f32[8,8,128]{2,1,0:T(8,128)S(1)} %get-tuple-element.14.before_ref), custom_call_target="tpu_custom_call" | custom-call | tf_op jit(solution)/shard_map/forces/pallas_call | solution.py:330
  (1 shorter events, 0.0 us)

commit v5 on v4

--- a/solution.py
+++ b/solution.py
@@ -8,7 +8,7 @@
 from jax.sharding import PartitionSpec as P
 
 AXES = ("gx", "gy", "gz")
-FIRST_PAIRS = (1, 0, 0)
+FIRST_PAIRS = (0, 0, 0)
 CUT = 144.0
 WIDTH = 44.0
 UNIT = 1.0 / math.sqrt(WIDTH)
@@ -29,7 +29,11 @@
 
 def early_stages():
     x, y, z = [lax.axis_index(name) for name in AXES]
-    return jnp.logical_and(x == 0, y + z > 0), x == 1
+    last = lax.axis_size("gy") - 1
+    corner = jnp.maximum(x, jnp.maximum(y, z)) < 2
+    beside = jnp.logical_and(x < 3, jnp.logical_or(y < 3, y == last))
+    first = jnp.logical_and(corner, x + y + z > 0)
+    return first, jnp.logical_and(jnp.logical_or(x == 0, beside), jnp.logical_not(corner))
 
 
 def free_cells(relation, fixed, choices):

time: 49.2 us -> 47.6 us (0.967)
  the two profiles are of different devices: /device:TPU:27 before, /device:TPU:1 now
where the time goes in v5:
time: 47.6 us; the launch traced here: 47.2 us
  blocking collectives  28.4 us (60%)
  Pallas kernels  18.8 us (39%)
    all_to_all x1, blocking collectives, per_device(): lax.all_to_all(send, AXES, 0, 0, axis_index_groups=swap_groups(sizes, FIR...  14.4 us
    all_to_all x1, blocking collectives, per_device(): lax.all_to_all(send, AXES, 0, 0, axis_index_groups=swap_groups(sizes, [1...  14.1 us
    pallas_call x1, Pallas kernels, per_device(): pl.pallas_call(force_kernel, out_shape=jax.ShapeDtypeStruct((3, 2, 2, 2,...  10.9 us
    pallas_call x1, Pallas kernels, per_device(): pl.pallas_call(atoms_kernel, out_shape=(part_shape, pltpu.VMEM((8, 4, 8,...  7.79 us

profile of v5, /device:TPU:1, one launch (start us, length us, event | category | flops | bytes accessed | tf_op | source)
XLA Modules:
  0.0 47.2 jit_solution(3848323197828497866)
XLA Ops:
  0.0 7.8 %atoms.1 = (f32[8,8,128]{2,1,0:T(8,128)S(1)}, f32[8,4,8,128]{3,2,1,0:T(8,128)S(1)}, f32[8,8,128]{2,1,0:T(8,128)S(1)}) custom-call(f32[3,2,2,2,128]{4,3,2,1,0:T(2,128)} %pos_ref.1, f32[2,2,2,128]{3,2,1,0:T(2,128)} %charge_ref.1, s32[2,2,2,128]{3,2,1,0:T(2,128)} %type_ref.1, s32[2,2,2]{2,1,0:T(2,128)} %count_ref.1, f32[1,128]{1,0:T(1,128)} %bitcast.2, ...), custom_call_target="tpu_custom_call" | custom-call | tf_op jit(solution)/shard_map/atoms/pallas_call | solution.py:316
  7.8 14.4 %all_to_all.10.got_ref.even_ref = f32[8,4,8,128]{3,2,1,0:T(8,128)S(1)} all-to-all(f32[8,4,8,128]{3,2,1,0:T(8,128)S(1)} %get-tuple-element.11), channel_id=1, replica_groups={{0,1,4,5,64,65,68,69},{2,3,6,7,66,67,70,71},{8,9,12,13,72,73,76,77},{10..., dimensions={0} | all-to-all | bytes 262144 | tf_op jit(solution)/shard_map/all_to_all | solution.py:324
  22.2 14.1 %all_to_all.11.odd_ref = f32[8,9,8,128]{3,2,1,0:T(8,128)S(1)} all-to-all(f32[8,9,8,128]{3,2,1,0:T(8,128)S(1)} %get-tuple-element.13), channel_id=1, replica_groups={{69,70,73,74,133,134,137,138},{71,68,75,72,135,132,139,136},{77,78,81,8..., dimensions={0} | all-to-all | bytes 589824 | tf_op jit(solution)/shard_map/all_to_all | solution.py:333
  36.3 10.9 %forces.1 = f32[3,2,2,2,128]{4,3,2,1,0:T(2,128)} custom-call(f32[8,8,128]{2,1,0:T(8,128)S(1)} %get-tuple-element.10.own_ref, f32[8,4,8,128]{3,2,1,0:T(8,128)S(1)} %all_to_all.10.got_ref.even_ref, f32[8,9,8,128]{3,2,1,0:T(8,128)S(1)} %all_to_all.11.odd_ref, f32[8,8,128]{2,1,0:T(8,128)S(1)} %get-tuple-element.14.before_ref), custom_call_target="tpu_custom_call" | custom-call | tf_op jit(solution)/shard_map/forces/pallas_call | solution.py:334
  (1 shorter events, 0.0 us)

commit v6 on v5

--- a/solution.py
+++ b/solution.py
@@ -41,7 +41,33 @@
     return [(x, y, z) for x in spans[0] for y in spans[1] for z in spans[2]]
 
 
-def atoms_kernel(pos_ref, charge_ref, type_ref, count_ref, sigma_ref, eps_ref, pair_ref, own_ref, send_ref, part_ref, rows_ref, kinds_ref, codes_ref, *work):
+def shipped(own_ref, cell):
+    tile = own_ref[cell]
+    return [(0, tile[0:4, :]), (4, tile[7:8, :])], tile[META_ROW:META_ROW + 1, :]
+
+
+def pack(send_ref, slot, most, cells):
+    lane = lax.broadcasted_iota(jnp.int32, (1, 128), 1)
+    flags = None
+    for n, (pieces, meta) in enumerate(cells):
+        for row, piece in pieces:
+            send_ref[slot, 5 * n + row:5 * n + row + piece.shape[0], :] = piece
+        meta = jnp.where(lane < 32, meta, 0.0)
+        flags = meta if n % 4 == 0 else flags + pltpu.roll(meta, 32 * (n % 4), axis=1)
+        if n % 4 == 3 or n == len(cells) - 1:
+            send_ref[slot, 5 * most + n // 4:5 * most + n // 4 + 1, :] = flags
+
+
+def unpack(got_ref, slot, most, n):
+    tile = got_ref[slot, 5 * n:5 * n + 8, :]
+    meta = got_ref[slot, 5 * most + n // 4:5 * most + n // 4 + 1, :]
+    if n % 4:
+        meta = pltpu.roll(meta, 128 - 32 * (n % 4), axis=1)
+    row = lax.broadcasted_iota(jnp.int32, (8, 128), 0)
+    return jnp.where(row == 5, jnp.broadcast_to(meta, (8, 128)), tile)
+
+
+def atoms_kernel(pos_ref, charge_ref, type_ref, count_ref, sigma_ref, eps_ref, pair_ref, own_ref, send_ref, part_ref, table_ref, rows_ref, kinds_ref, codes_ref, *work):
     for i in range(2):
         for j in range(2):
             at = pl.ds(4 * i + 2 * j, 2)
@@ -63,6 +89,7 @@
     kinds = kinds_ref[...]
     sigma = jnp.broadcast_to(sigma_ref[...] * (0.5 * UNIT), (8, 128))
     depth = jnp.broadcast_to(jnp.sqrt(eps_ref[...]) * DEPTH_UNIT, (8, 128))
+    table_ref[...] = jnp.where(cell == 4, sigma, jnp.where(cell == 5, depth, 0.0))
     sigma = jnp.take_along_axis(sigma, kinds, axis=1, mode="promise_in_bounds")
     depth = jnp.take_along_axis(depth, kinds, axis=1, mode="promise_in_bounds")
 
@@ -84,7 +111,7 @@
     values.append(jnp.where(live, rows_ref[3] * CHARGE_UNIT, 0.0))
     values.append(jnp.where(live, sigma, 0.5 * UNIT))
     values.append(jnp.where(live, depth, 0.0))
-    values += [meta, jnp.zeros((8, 128), jnp.float32)]
+    values += [meta, kinds.astype(jnp.float32)]
     for r in range(8):
         own_ref[:, r, :] = values[r]
 
@@ -92,62 +119,77 @@
     toward = [1 - b for b in odd]
     for rel in RELATIONS:
         slot = sum(lax.bitwise_xor(odd[a], rel[a]) * (4, 2, 1)[a] for a in range(3))
-        for n, (x, y, z) in enumerate(free_cells(rel, toward, 2)):
-            send_ref[slot, n] = own_ref[4 * x + 2 * y + z]
+        pack(send_ref, slot, 4, [shipped(own_ref, 4 * x + 2 * y + z) for x, y, z in free_cells(rel, toward, 2)])
     part_ref[...] = jnp.zeros(part_ref.shape, jnp.float32)
 
     @pl.when(early_stages()[0])
     def _():
         work[1][...] = jnp.zeros(work[1].shape, jnp.int32)
-        place(work[0], work[1], odd, own_ref, None, None)
+        place(work[0], work[1], odd, table_ref, own_ref, None, None)
         cell_forces(part_ref, None, None, *work)
 
 
-def relay_kernel(own_ref, got_ref, before_ref, send_ref, part_ref, *work):
+def relay_kernel(own_ref, got_ref, before_ref, table_ref, send_ref, part_ref, tiles_ref, *work):
     odd = parities()
     for rel in RELATIONS:
+        slot = sum(lax.bitwise_xor(odd[a], rel[a]) * (4, 2, 1)[a] for a in range(3))
+        for n in range(2 ** (3 - sum(rel))):
+            tiles_ref[slot, n] = unpack(got_ref, slot, 4, n)
+    for rel in RELATIONS:
         slot = sum(lax.bitwise_xor(1 - odd[a], rel[a]) * (4, 2, 1)[a] for a in range(3))
-        for n, at in enumerate(free_cells(rel, odd, 3)):
+        cells = []
+        for at in free_cells(rel, odd, 3):
             far = [isinstance(p, int) and p == 2 for p in at]
             if not any(far):
-                send_ref[slot, n] = own_ref[4 * at[0] + 2 * at[1] + at[2]]
+                cells.append(shipped(own_ref, 4 * at[0] + 2 * at[1] + at[2]))
                 continue
             source = sum(lax.bitwise_xor(odd[a], int(far[a])) * (4, 2, 1)[a] for a in range(3))
             m = 0
             for a in range(3):
                 if not far[a]:
                     m = m * 2 + at[a]
-            send_ref[slot, n] = got_ref[source, m]
+            tile = tiles_ref[source, m]
+            cells.append(([(0, tile[0:5, :])], tile[5:6, :]))
+        pack(send_ref, slot, 9, cells)
     part_ref[...] = before_ref[...]
 
     @pl.when(early_stages()[1])
     def _():
         work[1][...] = jnp.zeros(work[1].shape, jnp.int32)
-        place(work[0], work[1], odd, own_ref, got_ref, None)
+        place(work[0], work[1], odd, table_ref, own_ref, got_ref, None)
         cell_forces(part_ref, None, None, *work)
 
 
-def place(ext_ref, meta_ref, odd, own_ref, even_ref, odd_ref, even_done=0):
+def place(ext_ref, meta_ref, odd, table_ref, own_ref, even_ref, odd_ref, even_done=0):
     spot = [[1, 2, 3 - 3 * odd[a], 3 * odd[a]] for a in range(3)]
     lane = lax.broadcasted_iota(jnp.int32, (1, 128), 1)
 
-    def put(at, tile, done):
+    row = lax.broadcasted_iota(jnp.int32, (8, 128), 0)
+
+    def arrived(got_ref, slot, most, n):
+        tile = unpack(got_ref, slot, most, n)
+        kinds = jnp.broadcast_to(tile[4:5, :], (8, 128)).astype(jnp.int32)
+        kinds = jnp.clip(kinds, 0, 127)
+        found = jnp.take_along_axis(table_ref[...], kinds, axis=1, mode="promise_in_bounds")
+        return jnp.where(row < 4, tile, found), tile[5:6, :]
+
+    def put(at, tile, meta, done):
         where = spot[0][at[0]] * 16 + spot[1][at[1]] * 4 + spot[2][at[2]]
         ext_ref[where] = tile
-        meta = tile[META_ROW:META_ROW + 1, :].astype(jnp.int32)
+        meta = meta.astype(jnp.int32)
         meta_ref[pl.ds(where, 1), :] = jnp.where(jnp.logical_and(lane != COUNT_LANE, done > 0), 0, meta)
 
     for c in range(8):
-        put((c // 4, c // 2 % 2, c % 2), own_ref[c], 0)
+        put((c // 4, c // 2 % 2, c % 2), own_ref[c], own_ref[c, META_ROW:META_ROW + 1, :], 0)
     for rel in RELATIONS:
         if even_ref is not None:
             slot = sum(lax.bitwise_xor(odd[a], rel[a]) * (4, 2, 1)[a] for a in range(3))
             for n, at in enumerate(free_cells(rel, (2, 2, 2), 2)):
-                put(at, even_ref[slot, n], even_done)
+                put(at, *arrived(even_ref, slot, 4, n), even_done)
         if odd_ref is not None:
             slot = sum(lax.bitwise_xor(1 - odd[a], rel[a]) * (4, 2, 1)[a] for a in range(3))
             for n, at in enumerate(free_cells(rel, (3, 3, 3), 3)):
-                put(at, odd_ref[slot, n], 0)
+                put(at, *arrived(odd_ref, slot, 9, n), 0)
 
 
 def pair_terms(home, other):
@@ -284,9 +326,9 @@
         rows_ref[c] = rows if before_ref is None else rows + before_ref[c]
 
 
-def force_kernel(own_ref, even_ref, odd_ref, before_ref, out_ref, rows_ref, *work):
+def force_kernel(own_ref, even_ref, odd_ref, before_ref, table_ref, out_ref, rows_ref, *work):
     first, second = early_stages()
-    place(work[0], work[1], parities(), own_ref, even_ref, odd_ref, jnp.where(second, 1, 0))
+    place(work[0], work[1], parities(), table_ref, own_ref, even_ref, odd_ref, jnp.where(second, 1, 0))
     cell_forces(rows_ref, before_ref, jnp.logical_or(first, second), *work)
     for c in range(8):
         for a in range(3):
@@ -313,32 +355,32 @@
     smem = pl.BlockSpec(memory_space=pltpu.SMEM)
     part_shape = pltpu.VMEM((8, 8, 128), f32)
     keep = lambda x: pltpu.with_memory_space_constraint(x, pltpu.VMEM)
-    own, send, part = pl.pallas_call(
+    own, send, part, table = pl.pallas_call(
         atoms_kernel,
-        out_shape=(part_shape, pltpu.VMEM((8, 4, 8, 128), f32), part_shape),
+        out_shape=(part_shape, pltpu.VMEM((8, 24, 128), f32), part_shape, pltpu.VMEM((8, 128), f32)),
         in_specs=[vmem, vmem, vmem, smem, vmem, vmem, vmem],
-        out_specs=(vmem, vmem, vmem),
+        out_specs=(vmem,) * 4,
         scratch_shapes=[pltpu.VMEM((4, 8, 128), f32), pltpu.VMEM((8, 128), jnp.int32), pltpu.VMEM((8, 256), jnp.int32)] + WORK,
         name="atoms",
     )(positions, charges, atom_types, atom_counts, type_sigma.reshape(1, -1), type_epsilon.reshape(1, -1), pair_list)
     even = lax.all_to_all(send, AXES, 0, 0, axis_index_groups=swap_groups(sizes, FIRST_PAIRS), tiled=True)
     send, part = pl.pallas_call(
         relay_kernel,
-        out_shape=(pltpu.VMEM((8, 9, 8, 128), f32), part_shape),
-        in_specs=[vmem, vmem, vmem],
+        out_shape=(pltpu.VMEM((8, 48, 128), f32), part_shape),
+        in_specs=[vmem] * 4,
         out_specs=(vmem, vmem),
-        scratch_shapes=WORK,
+        scratch_shapes=[pltpu.VMEM((8, 4, 8, 128), f32)] + WORK,
         name="relay",
-    )(keep(own), keep(even), keep(part))
+    )(keep(own), keep(even), keep(part), keep(table))
     odd = lax.all_to_all(send, AXES, 0, 0, axis_index_groups=swap_groups(sizes, [1 - start for start in FIRST_PAIRS]), tiled=True)
     return pl.pallas_call(
         force_kernel,
         out_shape=jax.ShapeDtypeStruct((3, 2, 2, 2, 128), f32),
-        in_specs=[vmem] * 4,
+        in_specs=[vmem] * 5,
         out_specs=vmem,
         scratch_shapes=[pltpu.VMEM((8, 8, 128), f32)] + WORK,
         name="forces",
-    )(keep(own), keep(even), keep(odd), keep(part))
+    )(keep(own), keep(even), keep(odd), keep(part), keep(table))
 
 
 def solution(mesh):

time: 47.6 us -> 47.2 us (level); the launches traced: 47.2 us -> 47.8 us
  Pallas kernels: 18.8 us -> 22.7 us
  blocking collectives: 28.4 us -> 25.1 us
    pallas_call x1, Pallas kernels: 10.9 us -> 13 us  [per_device(): pl.pallas_call(force_kernel, out_shape=jax.ShapeDtypeStruct((3, 2, 2, 2,...]
    pallas_call x2, Pallas kernels: 7.82 us -> 9.68 us  [the longest x1 9.48 us: per_device(): pl.pallas_call(atoms_kernel, out_shape=(part_shape, pltpu.VMEM((8, 24, 12...]
    all_to_all x1, blocking collectives: 14.4 us -> 12.5 us  [per_device(): lax.all_to_all(send, AXES, 0, 0, axis_index_groups=swap_groups(sizes, FIR...]
    all_to_all x1, blocking collectives: 14.1 us -> 12.6 us  [per_device(): lax.all_to_all(send, AXES, 0, 0, axis_index_groups=swap_groups(sizes, [1...]
where the time goes in v6:
time: 47.2 us; the launch traced here: 47.8 us
  blocking collectives  25.1 us (53%)
  Pallas kernels  22.7 us (48%)
    pallas_call x1, Pallas kernels, per_device(): pl.pallas_call(force_kernel, out_shape=jax.ShapeDtypeStruct((3, 2, 2, 2,...  13 us
    all_to_all x1, blocking collectives, per_device(): lax.all_to_all(send, AXES, 0, 0, axis_index_groups=swap_groups(sizes, [1...  12.6 us
    all_to_all x1, blocking collectives, per_device(): lax.all_to_all(send, AXES, 0, 0, axis_index_groups=swap_groups(sizes, FIR...  12.5 us
    pallas_call x1, Pallas kernels, per_device(): pl.pallas_call(atoms_kernel, out_shape=(part_shape, pltpu.VMEM((8, 24, 12...  9.48 us

profile of v6, /device:TPU:1, one launch (start us, length us, event | category | flops | bytes accessed | tf_op | source)
XLA Modules:
  0.0 47.8 jit_solution(227576217741400791)
XLA Ops:
  0.0 9.5 %atoms.1 = (f32[8,8,128]{2,1,0:T(8,128)S(1)}, f32[8,24,128]{2,1,0:T(8,128)S(1)}, f32[8,8,128]{2,1,0:T(8,128)S(1)}, f32[8,128]{1,0:T(8,128)S(1)}) custom-call(f32[3,2,2,2,128]{4,3,2,1,0:T(2,128)} %pos_ref.1, f32[2,2,2,128]{3,2,1,0:T(2,128)} %charge_ref.1, s32[2,2,2,128]{3,2,1,0:T(2,128)} %type_ref.1, s32[2,2,2]{2,1,0:T(2,128)} %count_ref.1, ...), custom_call_target="tpu_custom_call" | custom-call | tf_op jit(solution)/shard_map/atoms/pallas_call | solution.py:358
  9.5 12.5 %all_to_all.10.got_ref.even_ref = f32[8,24,128]{2,1,0:T(8,128)S(1)} all-to-all(f32[8,24,128]{2,1,0:T(8,128)S(1)} %get-tuple-element.12), channel_id=1, replica_groups={{0,1,4,5,64,65,68,69},{2,3,6,7,66,67,70,71},{8,9,12,13,72,73,76,77},{10..., dimensions={0} | all-to-all | bytes 196608 | tf_op jit(solution)/shard_map/all_to_all | solution.py:366
  22.0 0.2 relay.1
  22.2 12.6 %all_to_all.11.odd_ref = f32[8,48,128]{2,1,0:T(8,128)S(1)} all-to-all(f32[8,48,128]{2,1,0:T(8,128)S(1)} %get-tuple-element.15), channel_id=1, replica_groups={{69,70,73,74,133,134,137,138},{71,68,75,72,135,132,139,136},{77,78,81,8..., dimensions={0} | all-to-all | bytes 393216 | tf_op jit(solution)/shard_map/all_to_all | solution.py:375
  34.8 13.0 %forces.1 = f32[3,2,2,2,128]{4,3,2,1,0:T(2,128)} custom-call(f32[8,8,128]{2,1,0:T(8,128)S(1)} %get-tuple-element.11.own_ref, f32[8,24,128]{2,1,0:T(8,128)S(1)} %all_to_all.10.got_ref.even_ref, f32[8,48,128]{2,1,0:T(8,128)S(1)} %all_to_all.11.odd_ref, f32[8,8,128]{2,1,0:T(8,128)S(1)} %get-tuple-element.16.before_ref, f32[8,128]{1,0:T(8,128)S(1)} %get-tuple-element.14.table_ref), custom_call_target="tpu_custom_call" | custom-call | tf_op jit(solution)/shard_map/forces/pallas_call | solution.py:376
